TPU v7x, 32 devices: a whole 2x2x4 slice. The times are simulated.
32 devices in a mesh: cols: 8 (over y, x, core), vars: 4 (over z).
Axes of the slice: x: 2, y: 2, z: 4, core: 2. Of those that a mesh axis runs over, the one named last changes fastest.
Arguments:
- model_state: float32 [128, 4, 16, 72], P(('cols', 'vars')), may hold values from -6 to 6
- cloud_state: float32 [4, 50, 65536], P(None, None, ('cols', 'vars')), may hold values from -6 to 6
- neighbor: int32 [128, 4], P(('cols', 'vars')), may hold values from 0 to 127, as said below
- facing_edge: int32 [128, 4], P(('cols', 'vars')), may hold values from 0 to 3, as said below
- column_order: int32 [8, 256], P('cols'), may hold values from 0 to 255, each once within a row
- model_to_cloud_levels: float32 [50, 72], replicated, may hold values from -0.75 to 0.75
- cloud_to_model_levels: float32 [72, 50], replicated, may hold values from -0.875 to 0.875
Outputs:
- model_next: float32 [128, 4, 16, 72], P(('cols', 'vars'))
- cloud_next: float32 [4, 50, 65536], P(None, None, ('cols', 'vars'))
Inputs may be any that keep to these rules, and one draw needn't show every extreme that they name: neighbor[e,j] is the element across edge j of element e; it lies in the same block of 4 consecutive elements as e or in one of the two blocks beside it, the first and last blocks counting as beside each other. Neighbours are mutual: if edge j of e faces edge f = facing_edge[e,j] of b, then edge f of b faces edge j of e. facing_edge[e,j] is the edge of neighbor[e,j] that edge j of e faces; the shared edge's nodes run in opposite orders in the two elements. `column_order`: each row is a permutation.
All inputs are finite; a program needn't handle non-finite values.
Results may differ from a plain program's by a relative error of at most 0.0003.
Values sent between devices are 32-bit elements; how exact they have to be, the bound alone decides.
No kernel may reach another device: no remote copies, remote signals or barrier semaphores. Data moves between devices by JAX's collectives and lax.ppermute only.
A program may use at most 128 MiB of HBM per device.

v0:
```python
import jax
import jax.numpy as jnp
import numpy as np
from jax import lax
from jax.sharding import PartitionSpec as P

CCOL = 32


TOP_LEVEL_INDEX = lax.Precision.HIGHEST
VISCOSITY = 0.01
DRIFT = 0.05
PENALTY = 0.5
TIME_STEP = 0.5
CLOUD_ADVECT = 0.25
CLOUD_DIFFUSE = 0.1
CONDENSE_RATE = 0.3
SATURATION_BASE = 0.5
SATURATION_SLOPE = 0.3
RETAIN = 0.8
EDGE_NODES = [[0, 1, 2, 3], [3, 7, 11, 15], [15, 14, 13, 12], [12, 8, 4, 0]]


def padded_2(block, sides, width):
    for axis, dim in sides:
        count = lax.axis_size(axis)
        forward = [(i, i + 1) for i in range(count - 1)]
        forward.append((count - 1, 0))
        backward = [(target, source) for source, target in forward]
        low = lax.ppermute(
            lax.slice_in_dim(block, block.shape[dim] - width, None, axis=dim), axis, forward
        )
        high = lax.ppermute(lax.slice_in_dim(block, 0, width, axis=dim), axis, backward)
        block = jnp.concatenate([low, block, high], axis=dim)
    return block


def lobatto_derivative():
    points = np.array([-1.0, -1.0 / np.sqrt(5.0), 1.0 / np.sqrt(5.0), 1.0])
    derivative = np.zeros((4, 4))
    for target in range(4):
        for source in range(4):
            if target != source:
                weight_target = np.prod(
                    [points[target] - points[middle] for middle in range(4) if middle != target]
                )
                weight_source = np.prod(
                    [points[source] - points[middle] for middle in range(4) if middle != source]
                )
                derivative[target, source] = weight_target / (
                    weight_source * (points[target] - points[source])
                )
        derivative[target, target] = np.sum(
            [1.0 / (points[target] - points[middle]) for middle in range(4) if middle != target]
        )
    return derivative


def node_operators():
    derivative = lobatto_derivative()
    identity = np.eye(4)
    along_first = np.kron(identity, derivative)
    along_second = np.kron(derivative, identity)
    laplace = along_first @ along_first + along_second @ along_second
    return (jnp.asarray(along_first, jnp.float32), jnp.asarray(laplace, jnp.float32))


def edge_tables():
    source = np.zeros((4, 4, 16))
    target = np.zeros((4, 4, 16))
    for edge in range(4):
        for place in range(4):
            source[edge, place, EDGE_NODES[edge][3 - place]] = 1.0
            target[edge, place, EDGE_NODES[edge][place]] = 1.0
    return (jnp.asarray(source, jnp.float32), jnp.asarray(target, jnp.float32))


def tendency_of(own_elems, far_list, facing_edge):
    along_first, laplace = node_operators()
    source, target = edge_tables()
    diffused = jnp.einsum("mn,evnl->evml", laplace, own_elems, precision=TOP_LEVEL_INDEX)
    slope = jnp.einsum("mn,evnl->evml", along_first, own_elems, precision=TOP_LEVEL_INDEX)
    result = VISCOSITY * diffused - DRIFT * own_elems[:, 3:4] * slope
    penalty_sum = jnp.zeros_like(own_elems)
    for edge in range(4):
        choose = (facing_edge[:, edge][:, None] == jnp.arange(4, dtype=jnp.int32)[None, :]).astype(
            jnp.float32
        )
        picker = jnp.einsum("ef,ftn->etn", choose, source, precision=TOP_LEVEL_INDEX)
        facing = jnp.einsum("etn,evnl->evtl", picker, far_list[edge], precision=TOP_LEVEL_INDEX)
        inside = jnp.einsum("tn,evnl->evtl", target[edge], own_elems, precision=TOP_LEVEL_INDEX)
        penalty_sum = penalty_sum + jnp.einsum(
            "tm,evtl->evml", target[edge], facing - inside, precision=TOP_LEVEL_INDEX
        )
    return result + PENALTY * penalty_sum


def cloud_step(cloud_fields, applied_forcing):
    width = cloud_fields.shape[2]
    model_cols = width // CCOL
    within = jnp.arange(width, dtype=jnp.int32) % CCOL
    ahead = jnp.where(
        within == CCOL - 1,
        jnp.roll(cloud_fields, CCOL - 1, axis=2),
        jnp.roll(cloud_fields, -1, axis=2),
    )
    behind = jnp.where(
        within == 0, jnp.roll(cloud_fields, -(CCOL - 1), axis=2), jnp.roll(cloud_fields, 1, axis=2)
    )
    advect = -CLOUD_ADVECT * cloud_fields[3:4] * (ahead - behind)
    padded = jnp.pad(cloud_fields, ((0, 0), (1, 1), (0, 0)))
    diffuse = CLOUD_DIFFUSE * (padded[:, 2:] - 2.0 * cloud_fields + padded[:, :-2])
    spread = jnp.repeat(applied_forcing, CCOL, axis=2)
    moved = cloud_fields + TIME_STEP * (advect + diffuse + spread)
    saturation = SATURATION_BASE * jnp.exp(SATURATION_SLOPE * moved[0])
    condensed = CONDENSE_RATE * jax.nn.softplus(moved[1] - saturation)
    updated = jnp.stack(
        [moved[0] + condensed, moved[1] - condensed, RETAIN * moved[2] + condensed, moved[3]]
    )
    owner_col = jnp.arange(width, dtype=jnp.int32) // CCOL
    pooling = (owner_col[:, None] == jnp.arange(model_cols, dtype=jnp.int32)[None, :]).astype(
        jnp.float32
    )
    state_increment = jnp.einsum(
        "vzk,kc->vzc", updated - cloud_fields, pooling, precision=TOP_LEVEL_INDEX
    ) / (CCOL * TIME_STEP)
    return (updated, state_increment)


def to_owners(positioned_blocks):
    return lax.all_to_all(positioned_blocks, "vars", split_axis=2, concat_axis=0, tiled=True)


def to_block(values):
    return lax.all_to_all(values, "vars", split_axis=0, concat_axis=2, tiled=True)


def shards(
    model_state,
    cloud_state,
    neighbor,
    facing_edge,
    column_order,
    model_to_cloud_levels,
    cloud_to_model_levels,
):
    elements = model_state.shape[0]
    var_count = model_state.shape[1]
    levels = model_state.shape[3]
    element_count = elements * lax.axis_size(("cols", "vars"))
    offset = lax.axis_index(("cols", "vars")) * elements
    widened = padded_2(model_state, ((("cols", "vars"), 0),), elements)
    local_index = (neighbor - offset + elements) % element_count
    far_list = [jnp.take(widened, local_index[:, edge], axis=0) for edge in range(4)]
    tendency = tendency_of(model_state, far_list, facing_edge)
    outgoing = jnp.transpose(tendency, (1, 3, 0, 2)).reshape(var_count, levels, elements * 16)
    order_row = column_order[0]
    arrived = lax.all_to_all(
        lax.all_to_all(outgoing, "vars", split_axis=0, concat_axis=2, tiled=True),
        "cols",
        split_axis=2,
        concat_axis=2,
        tiled=True,
    )
    positioned_blocks = jnp.take(arrived, order_row, axis=2)
    locally_owned = to_owners(positioned_blocks)
    applied_forcing = jnp.einsum(
        "dg,wgk->wdk", model_to_cloud_levels, locally_owned, precision=TOP_LEVEL_INDEX
    )
    updated, state_increment = cloud_step(cloud_state, applied_forcing)
    returned_output = jnp.einsum(
        "xi,yie->yxe", cloud_to_model_levels, state_increment, precision=TOP_LEVEL_INDEX
    )
    gathered = to_block(returned_output)
    slot_order = jnp.zeros_like(gathered).at[:, :, order_row].set(gathered)
    at_home = lax.all_to_all(
        lax.all_to_all(slot_order, "cols", split_axis=2, concat_axis=2, tiled=True),
        "vars",
        split_axis=2,
        concat_axis=0,
        tiled=True,
    )
    feedback = at_home.reshape(var_count, levels, elements, 16).transpose(2, 0, 3, 1)
    model_next = model_state + TIME_STEP * (tendency + feedback)
    return (model_next, updated)


def solution(mesh):
    placed = (
        P(("cols", "vars"), None, None, None),
        P(None, None, ("cols", "vars")),
        P(("cols", "vars"), None),
        P(("cols", "vars"), None),
        P("cols", None),
        P(),
        P(),
    )
    return jax.shard_map(
        shards,
        mesh=mesh,
        in_specs=placed,
        out_specs=(P(("cols", "vars"), None, None, None), P(None, None, ("cols", "vars"))),
        check_vma=False,
    )
```

profile of v0, /device:TPU:0, one launch (start us, length us, event | category | flops | bytes accessed | tf_op | source)
XLA Modules:
  0.0 168.1 jit_solution(3794078743888842710)
XLA Ops:
  0.7 6.5 %collective-permute-start.1 = (f32[4,4,16,72]{3,2,1,0:T(8,128)}, f32[4,4,16,72]{3,2,1,0:T(8,128)}, u32[]{:S(2)}, u32[]{:S(2)}) collective-permute-start(f32[4,4,16,72]{3,2,1,0:T(8,128)} %param.13), channel_id=1, source_target_pairs={{1,0},{2,1},{3,2},{4,3},{5,4},{6,5},{7,6},{8,7},{9,8},{10,9},{11,1... | collective-permute-start | bytes 221192 | tf_op jit(solution)/shard_map/ppermute | solution.py:33
  7.1 0.7 add_select_fusion.2
  8.0 0.6 compare_and_fusion
  8.6 0.6 compare_select_fusion.3
  9.2 0.6 compare_and_fusion.2
  10.3 1.4 fusion.37
  11.7 1.7 %fusion.70 = (f32[4,50,1]{2,0,1:T(4,128)}, f32[4,50,1]{2,0,1:T(4,128)}) fusion(f32[4,50,2048]{2,0,1:T(4,128)} %param.14), kind=kLoop, calls=%fused_computation.145 | loop fusion | bytes 3200 | tf_op jit(solution)/shard_map/jit(_roll_static)/slice | solution.py:105
  13.4 1.6 fusion.71
  15.0 2.6 %slice.111 = f32[1,50,2048]{2,0,1:T(1,128)} slice(f32[4,50,2048]{2,0,1:T(4,128)} %param.14), slice={[3:4], [0:50], [0:2048]} | slice | bytes 819200 | tf_op jit(solution)/shard_map/slice | solution.py:110
  17.7 2.7 %fusion.69 = (f32[4,50,2047]{2,0,1:T(4,128)}, f32[4,50,2047]{2,0,1:T(4,128)}) fusion(f32[4,50,2048]{2,0,1:T(4,128)S(1)} %copy-done.1), kind=kLoop, calls=%fused_computation.144 | loop fusion | bytes 6550400 | tf_op jit(solution)/shard_map/jit(_roll_static)/slice | solution.py:105
  20.4 2.2 %fusion.72 = (f32[4,50,2017]{2,0,1:T(4,128)S(1)}, f32[4,50,2017]{2,0,1:T(4,128)}) fusion(f32[4,50,2048]{2,0,1:T(4,128)S(1)} %copy-done.1), kind=kLoop, calls=%fused_computation.147 | loop fusion | bytes 6454400 | tf_op jit(solution)/shard_map/jit(_roll_static)/slice | solution.py:104
  22.6 3.3 %copy.49 = f32[4,50,2048]{1,2,0:T(8,128)} copy(f32[4,50,2048]{2,0,1:T(4,128)S(1)} %copy-done.1) | data formatting | bytes 3276800 | tf_op args[1]
  25.9 1.3 compare_select_fusion.1
  27.2 1.2 compare_and_fusion.4
  28.6 1.3 pad_clamp_fusion.3
  29.9 0.6 pad_clamp_fusion.1
  30.4 1.2 pad_clamp_fusion.4
  31.7 0.9 convolution_bitcast_fusion.6
  32.5 1.5 convolution_bitcast_fusion.8
  34.0 1.5 convolution_bitcast_fusion.9
  35.5 1.5 convolution_bitcast_fusion.7
  37.0 1.5 convolution_bitcast_fusion.5
  38.5 1.5 convolution_bitcast_fusion.4
  40.0 1.5 convolution_bitcast_fusion.3
  41.4 1.5 convolution_bitcast_fusion.2
  42.9 1.6 convolution_multiply_fusion
  44.5 0.9 fusion.73
  45.4 1.0 fusion.16
  46.4 2.4 %copy.38 = f32[50,2048]{0,1:T(8,128)} copy(f32[50,2048]{1,0:T(8,128)} %fusion.16) | data formatting | bytes 819200 | tf_op jit(solution)/shard_map/mul | solution.py:110
  48.8 4.7 %pad_maximum_fusion.1 = (f32[4,50,2048]{2,0,1:T(4,128)}, f32[4,50,2048]{2,0,1:T(4,128)}) fusion(f32[4,50,1]{2,0,1:T(4,128)} %get-tuple-element.21, f32[4,50,2047]{2,0,1:T(4,128)} %get-tuple-element.19, f32[4,50,2047]{2,0,1:T(4,128)} %get-tuple-element.20, f32[4,50,1]{2,0,1:T(4,128)} %get-tuple-element.22), kind=kLoop, calls=%fused_computation.13 | loop fusion | flops 819200 | bytes 6553600 | tf_op jit(solution)/shard_map/jit(_roll_static)/concatenate | solution.py:105
  53.5 4.4 %copy.40 = f32[4,50,2048]{1,2,0:T(8,128)} copy(f32[4,50,2048]{2,0,1:T(4,128)} %get-tuple-element.41) | data formatting | bytes 3276800 | tf_op jit(solution)/shard_map/jit(_roll_static)/concatenate | solution.py:105
  57.9 4.3 %pad_maximum_fusion = (f32[4,50,2048]{2,0,1:T(4,128)}, f32[4,50,2048]{2,0,1:T(4,128)}) fusion(f32[4,50,2017]{2,0,1:T(4,128)S(1)} %get-tuple-element.25, f32[4,50,31]{2,0,1:T(4,128)S(1)} %get-tuple-element.23, f32[4,50,31]{2,0,1:T(4,128)} %get-tuple-element.24, f32[4,50,2017]{2,0,1:T(4,128)} %get-tuple-element.26), kind=kLoop, calls=%fused_computation.12 | loop fusion | flops 819200 | bytes 6553600 | tf_op jit(solution)/shard_map/jit(_roll_static)/concatenate | solution.py:104
  62.2 4.4 %copy.39 = f32[4,50,2048]{1,2,0:T(8,128)} copy(f32[4,50,2048]{2,0,1:T(4,128)} %get-tuple-element.39) | data formatting | bytes 3276800 | tf_op jit(solution)/shard_map/jit(_roll_static)/concatenate | solution.py:104
  66.6 4.5 %copy.41 = f32[4,50,2048]{1,2,0:T(8,128)} copy(f32[4,50,2048]{2,0,1:T(4,128)} %get-tuple-element.40) | data formatting | bytes 3276800 | tf_op jit(solution)/shard_map/jit(_roll_static)/concatenate | solution.py:108
  71.2 3.3 %copy.42 = f32[4,50,2048]{1,2,0:T(8,128)} copy(f32[4,50,2048]{2,0,1:T(4,128)S(1)} %copy-done.3) | data formatting | bytes 3276800 | tf_op jit(solution)/shard_map/jit(_roll_static)/concatenate | solution.py:108
  74.6 0.9 constant_dynamic-update-slice_fusion.2
  75.6 1.0 constant_dynamic-update-slice_fusion
  76.6 0.7 gather_fusion.4
  77.3 0.6 gather_fusion.3
  77.9 0.7 gather_fusion.2
  78.6 0.7 gather_fusion.1
  81.5 1.0 bitcast_add_fusion.2
  82.5 0.7 copy.45
  83.2 3.9 %all-to-all-start = ((f32[4,72,64]{1,2,0:T(8,128)}), f32[4,72,64]{1,2,0:T(8,128)}, u32[]{:S(2)}, u32[]{:S(2)}) async-start(f32[4,72,64]{1,2,0:T(8,128)} %bitcast.40), calls=%async_computation | async-start | bytes 262144 | tf_op jit(solution)/shard_map/all_to_all | solution.py:159
  87.1 6.4 %all-to-all-done = f32[4,72,64]{1,2,0:T(8,128)} async-done(((f32[4,72,64]{1,2,0:T(8,128)}), f32[4,72,64]{1,2,0:T(8,128)}, u32[]{:S(2)}, u32[]{:S(2)}) %all-to-all-start) | async-done | bytes 73760 | tf_op jit(solution)/shard_map/all_to_all | solution.py:159
  93.6 3.4 %all-to-all-start.1 = ((f32[1,72,256]{1,0,2:T(1,128)}), f32[1,72,256]{1,0,2:T(1,128)S(1)}, u32[]{:S(2)}, u32[]{:S(2)}) async-start(f32[1,72,256]{1,0,2:T(1,128)} %bitcast.44), calls=%async_computation.1 | async-start | bytes 262144 | tf_op jit(solution)/shard_map/all_to_all | solution.py:158
  97.0 5.4 %all-to-all-done.1 = f32[1,72,256]{1,0,2:T(1,128)S(1)} async-done(((f32[1,72,256]{1,0,2:T(1,128)}), f32[1,72,256]{1,0,2:T(1,128)S(1)}, u32[]{:S(2)}, u32[]{:S(2)}) %all-to-all-start.1) | async-done | bytes 73760 | tf_op jit(solution)/shard_map/all_to_all | solution.py:158
  102.4 0.7 gather_fusion
  103.1 0.8 bitcast_select_fusion
  103.9 3.5 %all-to-all-start.2 = ((f32[1,72,256]{1,0,2:T(1,128)}), f32[1,72,256]{1,0,2:T(1,128)S(1)}, u32[]{:S(2)}, u32[]{:S(2)}) async-start(f32[1,72,256]{1,0,2:T(1,128)} %bitcast.48), calls=%async_computation.2 | async-start | bytes 262144 | tf_op jit(solution)/shard_map/all_to_all | solution.py:131
  107.4 6.0 %all-to-all-done.2 = f32[1,72,256]{1,0,2:T(1,128)S(1)} async-done(((f32[1,72,256]{1,0,2:T(1,128)}), f32[1,72,256]{1,0,2:T(1,128)S(1)}, u32[]{:S(2)}, u32[]{:S(2)}) %all-to-all-start.2) | async-done | bytes 73760 | tf_op jit(solution)/shard_map/all_to_all | solution.py:131
  114.0 11.3 %fusion.1 = f32[4,50,2048]{1,2,0:T(8,128)S(1)} fusion(f32[4,50,2048]{1,2,0:T(8,128)} %copy.49, f32[4,50,2048]{1,2,0:T(8,128)} %copy.41, f32[4,50,2048]{1,2,0:T(8,128)} %copy.42, f32[4,50,2048]{1,2,0:T(8,128)} %copy.39, f32[4,50,2048]{1,2,0:T(8,128)} %copy.40, f32[4,50,64]{1,2,0:T(8,128)S(1)} %copy.48, f32[50,2048]{0,1:T(8,128)S(1)} %copy-done.4, ...), kind=kLoop, calls=%fused_computation.8 | loop fusion | flops 4915200 | bytes 10295296 | tf_op jit(solution)/shard_map/add | solution.py:114
  125.4 2.3 %slice_add_fusion = (f32[1,50,2048]{1,2,0:T(8,128)}, f32[1,50,2048]{1,2,0:T(8,128)}, f32[1,50,2048]{1,2,0:T(8,128)}, f32[1,50,2048]{1,2,0:T(8,128)S(1)}) fusion(f32[4,50,2048]{1,2,0:T(8,128)S(1)} %fusion.1), kind=kLoop, calls=%fused_computation.45 | loop fusion | flops 1433600 | bytes 3276800 | tf_op jit(solution)/shard_map/add | solution.py:118
  127.6 1.5 copy.50
  129.1 2.1 %copy.53 = f32[1,50,2048]{2,0,1:T(1,128)} copy(f32[1,50,2048]{1,2,0:T(8,128)} %get-tuple-element.16) | data formatting | bytes 819200 | tf_op jit(solution)/shard_map/slice | solution.py:118
  131.3 2.1 %copy.52 = f32[1,50,2048]{2,0,1:T(1,128)} copy(f32[1,50,2048]{1,2,0:T(8,128)} %get-tuple-element.17) | data formatting | bytes 819200 | tf_op jit(solution)/shard_map/add | solution.py:118
  133.4 1.2 copy.51
  134.6 4.4 %fusion.68 = (f32[4,50,2048]{2,0,1:T(4,128)S(1)}, f32[4,50,2048]{2,0,1:T(4,128)}) fusion(f32[4,50,2048]{2,0,1:T(4,128)S(1)} %copy-done.1, f32[1,50,2048]{2,0,1:T(1,128)} %copy.53, f32[1,50,2048]{2,0,1:T(1,128)} %copy.52, f32[1,50,2048]{2,0,1:T(1,128)} %copy.51, f32[1,50,2048]{2,0,1:T(1,128)S(1)} %copy.50), kind=kLoop, calls=%fused_computation.143 | loop fusion | flops 1638400 | bytes 6553600 | tf_op jit(solution)/shard_map/sub | solution.py:125
  139.0 1.9 %fusion.5 = f32[4,50,64]{2,1,0:T(8,128)S(1)} fusion(f32[4,50,2048]{2,0,1:T(4,128)S(1)} %get-tuple-element.13, s32[2048]{0:T(1024)S(1)} %add_select_fusion), kind=kOutput, calls=%fused_computation.23 | convolution fusion | flops 314716672 | bytes 1697792 | tf_op jit(solution)/shard_map/vzk,kc->vzc/dot_general | solution.py:124
  141.3 8.4 %all_to_all.79 = f32[4,72,64]{1,2,0:T(8,128)S(1)} all-to-all(f32[4,72,64]{1,2,0:T(8,128)S(1)} %convolution_bitcast_fusion), channel_id=1, replica_groups=mesh['cols'=8,'vars'=4] {'vars'}, dimensions={0} | all-to-all | bytes 147456 | tf_op jit(solution)/shard_map/all_to_all | solution.py:135
  149.7 1.2 scatter_custom_fusion
  150.9 7.9 %all_to_all.80 = f32[1,72,256]{1,0,2:T(1,128)S(1)} all-to-all(f32[1,72,256]{1,0,2:T(1,128)S(1)} %bitcast.176), channel_id=1, replica_groups=mesh['cols'=8,'vars'=4] {'cols'}, dimensions={2} | all-to-all | bytes 147456 | tf_op jit(solution)/shard_map/all_to_all | solution.py:177
  158.8 8.5 %all_to_all.81 = f32[1,72,256]{1,0,2:T(1,128)S(1)} all-to-all(f32[1,72,256]{1,0,2:T(1,128)S(1)} %all_to_all.80), channel_id=1, replica_groups=mesh['cols'=8,'vars'=4] {'vars'}, dimensions={2} | all-to-all | bytes 147456 | tf_op jit(solution)/shard_map/all_to_all | solution.py:176
  167.4 0.7 fusion.19
  (85 shorter events, 4.2 us)
Async XLA Ops:
  0.6 140.3 %copy-start = (f32[72,50]{0,1:T(8,128)S(1)}, f32[72,50]{0,1:T(8,128)}, u32[]{:S(2)}) copy-start(f32[72,50]{0,1:T(8,128)} %param.19) | copy-start | bytes 43204
  0.6 17.0 %copy-start.1 = (f32[4,50,2048]{2,0,1:T(4,128)S(1)}, f32[4,50,2048]{2,0,1:T(4,128)}, u32[]{:S(2)}) copy-start(f32[4,50,2048]{2,0,1:T(4,128)} %param.14) | copy-start | bytes 4915204
  0.7 75.0 %collective-permute-start.1 = (f32[4,4,16,72]{3,2,1,0:T(8,128)}, f32[4,4,16,72]{3,2,1,0:T(8,128)}, u32[]{:S(2)}, u32[]{:S(2)}) collective-permute-start(f32[4,4,16,72]{3,2,1,0:T(8,128)} %param.13), channel_id=1, source_target_pairs={{1,0},{2,1},{3,2},{4,3},{5,4},{6,5},{7,6},{8,7},{9,8},{10,9},{11,1... | collective-permute-start | bytes 221192 | tf_op jit(solution)/shard_map/ppermute | solution.py:33
  7.1 67.5 %collective-permute-start = (f32[4,4,16,72]{3,2,1,0:T(8,128)}, f32[4,4,16,72]{3,2,1,0:T(8,128)}, u32[]{:S(2)}, u32[]{:S(2)}) collective-permute-start(f32[4,4,16,72]{3,2,1,0:T(8,128)} %param.13), channel_id=1, source_target_pairs={{0,1},{1,2},{2,3},{3,4},{4,5},{5,6},{6,7},{7,8},{8,9},{9,10},{10,1... | collective-permute-start | bytes 221192 | tf_op jit(solution)/shard_map/ppermute | solution.py:30
  22.6 5.8 %copy-start.15 = (s32[4,4]{1,0:T(4,128)S(1)}, s32[4,4]{1,0:T(4,128)}, u32[]{:S(2)}) copy-start(s32[4,4]{1,0:T(4,128)} %param.16) | copy-start | bytes 196
  22.6 14.4 %copy-start.2 = (f32[4,4,16,72]{3,2,1,0:T(8,128)S(1)}, f32[4,4,16,72]{3,2,1,0:T(8,128)}, u32[]{:S(2)}) copy-start(f32[4,4,16,72]{3,2,1,0:T(8,128)} %param.13) | copy-start | bytes 221188
  22.6 21.9 %copy-start.17 = (f32[16,16,1,1]{1,0,3,2:T(8,128)S(1)}, f32[16,16,1,1]{1,0,3,2:T(8,128)}, u32[]{:S(2)}) copy-start(f32[16,16,1,1]{1,0,3,2:T(8,128)} %constant.140) | copy-start | bytes 3076
  25.9 19.5 %copy-start.5 = (f32[1,50,2048]{2,0,1:T(1,128)S(1)}, f32[1,50,2048]{2,0,1:T(1,128)}, u32[]{:S(2)}) copy-start(f32[1,50,2048]{2,0,1:T(1,128)} %slice.111) | copy-start | bytes 1228804
  66.6 4.5 %copy-start.3 = (f32[4,50,2048]{2,0,1:T(4,128)S(1)}, f32[4,50,2048]{2,0,1:T(4,128)}, u32[]{:S(2)}) copy-start(f32[4,50,2048]{2,0,1:T(4,128)} %get-tuple-element.42) | copy-start | bytes 4915204
  71.1 3.4 %copy-start.30 = (s32[4]{0:T(128)S(1)}, s32[4]{0:T(128)}, u32[]{:S(2)}) copy-start(s32[4]{0:T(128)} %get-tuple-element.32) | copy-start | bytes 52
  74.5 4.8 %copy-start.14 = (f32[4,4,72,4]{2,3,1,0:T(4,128)S(1)}, f32[4,4,72,4]{2,3,1,0:T(4,128)}, u32[]{:S(2)}) copy-start(f32[4,4,72,4]{2,3,1,0:T(4,128)} %convolution_bitcast_fusion.5) | copy-start | bytes 55300
  74.5 4.8 %copy-start.20 = (f32[4,4,16,1]{2,0,1,3:T(4,128)S(1)}, f32[4,4,16,1]{2,0,1,3:T(4,128)}, u32[]{:S(2)}) copy-start(f32[4,4,16,1]{2,0,1,3:T(4,128)} %convolution_bitcast_fusion.9) | copy-start | bytes 3076
  74.5 4.8 %copy-start.29 = (pred[4]{0:T(512)(128)(4,1)S(1)}, pred[4]{0:T(512)(128)(4,1)}, u32[]{:S(2)}) copy-start(pred[4]{0:T(512)(128)(4,1)} %get-tuple-element.38) | copy-start | bytes 16
  74.5 5.1 %copy-start.24 = (f32[4,16,1,1]{1,0,3,2:T(4,128)S(1)}, f32[4,16,1,1]{1,0,3,2:T(4,128)}, u32[]{:S(2)}) copy-start(f32[4,16,1,1]{1,0,3,2:T(4,128)} %constant.141) | copy-start | bytes 772
  74.5 5.4 %copy-start.13 = (f32[4,4,72,4]{2,3,1,0:T(4,128)S(1)}, f32[4,4,72,4]{2,3,1,0:T(4,128)}, u32[]{:S(2)}) copy-start(f32[4,4,72,4]{2,3,1,0:T(4,128)} %convolution_bitcast_fusion.4) | copy-start | bytes 55300
  74.5 5.4 %copy-start.19 = (f32[4,4,16,1]{2,0,1,3:T(4,128)S(1)}, f32[4,4,16,1]{2,0,1,3:T(4,128)}, u32[]{:S(2)}) copy-start(f32[4,4,16,1]{2,0,1,3:T(4,128)} %convolution_bitcast_fusion.8) | copy-start | bytes 3076
  74.5 5.4 %copy-start.28 = (pred[4]{0:T(512)(128)(4,1)S(1)}, pred[4]{0:T(512)(128)(4,1)}, u32[]{:S(2)}) copy-start(pred[4]{0:T(512)(128)(4,1)} %get-tuple-element.37) | copy-start | bytes 16
  74.5 5.7 %copy-start.23 = (f32[4,16,1,1]{1,0,3,2:T(4,128)S(1)}, f32[4,16,1,1]{1,0,3,2:T(4,128)}, u32[]{:S(2)}) copy-start(f32[4,16,1,1]{1,0,3,2:T(4,128)} %constant.142) | copy-start | bytes 772
  74.5 6.0 %copy-start.12 = (f32[4,4,72,4]{2,3,1,0:T(4,128)S(1)}, f32[4,4,72,4]{2,3,1,0:T(4,128)}, u32[]{:S(2)}) copy-start(f32[4,4,72,4]{2,3,1,0:T(4,128)} %convolution_bitcast_fusion.3) | copy-start | bytes 55300
  74.5 6.0 %copy-start.18 = (f32[4,4,16,1]{2,0,1,3:T(4,128)S(1)}, f32[4,4,16,1]{2,0,1,3:T(4,128)}, u32[]{:S(2)}) copy-start(f32[4,4,16,1]{2,0,1,3:T(4,128)} %convolution_bitcast_fusion.7) | copy-start | bytes 3076
  74.5 6.0 %copy-start.27 = (pred[4]{0:T(512)(128)(4,1)S(1)}, pred[4]{0:T(512)(128)(4,1)}, u32[]{:S(2)}) copy-start(pred[4]{0:T(512)(128)(4,1)} %get-tuple-element.36) | copy-start | bytes 16
  74.5 6.3 %copy-start.22 = (f32[4,16,1,1]{1,0,3,2:T(4,128)S(1)}, f32[4,16,1,1]{1,0,3,2:T(4,128)}, u32[]{:S(2)}) copy-start(f32[4,16,1,1]{1,0,3,2:T(4,128)} %constant.143) | copy-start | bytes 772
  74.6 6.6 %copy-start.11 = (f32[4,4,72,4]{2,3,1,0:T(4,128)S(1)}, f32[4,4,72,4]{2,3,1,0:T(4,128)}, u32[]{:S(2)}) copy-start(f32[4,4,72,4]{2,3,1,0:T(4,128)} %convolution_bitcast_fusion.2) | copy-start | bytes 55300
  74.6 6.6 %copy-start.26 = (pred[4]{0:T(512)(128)(4,1)S(1)}, pred[4]{0:T(512)(128)(4,1)}, u32[]{:S(2)}) copy-start(pred[4]{0:T(512)(128)(4,1)} %get-tuple-element.35) | copy-start | bytes 16
  75.6 5.9 %copy-start.6 = (f32[16,4,4,72]{3,0,2,1:T(8,128)S(1)}, f32[16,4,4,72]{3,0,2,1:T(8,128)}, u32[]{:S(2)}) copy-start(f32[16,4,4,72]{3,0,2,1:T(8,128)} %convolution_multiply_fusion) | copy-start | bytes 221188
  75.6 5.9 %copy-start.7 = (f32[16,4,4,72]{3,0,2,1:T(8,128)S(1)}, f32[16,4,4,72]{3,0,2,1:T(8,128)}, u32[]{:S(2)}) copy-start(f32[16,4,4,72]{3,0,2,1:T(8,128)} %fusion.73) | copy-start | bytes 221188
  75.6 5.9 %copy-start.10 = (f32[72,4,16]{0,2,1:T(8,128)S(1)}, f32[72,4,16]{0,2,1:T(8,128)}, u32[]{:S(2)}) copy-start(f32[72,4,16]{0,2,1:T(8,128)} %get-tuple-element.28) | copy-start | bytes 55300
  75.6 5.9 %copy-start.21 = (f32[4,16,1,1]{1,0,3,2:T(4,128)S(1)}, f32[4,16,1,1]{1,0,3,2:T(4,128)}, u32[]{:S(2)}) copy-start(f32[4,16,1,1]{1,0,3,2:T(4,128)} %constant.144) | copy-start | bytes 772
  78.6 18.4 %copy-start.25 = (s32[256,1]{0,1:T(1,128)S(1)}, s32[256,1]{0,1:T(1,128)}, u32[]{:S(2)}) copy-start(s32[256,1]{0,1:T(1,128)} %compare_select_fusion.1) | copy-start | bytes 3076
  80.2 22.9 %copy-start.31 = (pred[256]{0:T(512)(128)(4,1)S(1)}, pred[256]{0:T(512)(128)(4,1)}, u32[]{:S(2)}) copy-start(pred[256]{0:T(512)(128)(4,1)} %compare_and_fusion.4) | copy-start | bytes 772
  80.9 32.6 %copy-start.16 = (f32[50,72]{1,0:T(8,128)S(1)}, f32[50,72]{1,0:T(8,128)}, u32[]{:S(2)}) copy-start(f32[50,72]{1,0:T(8,128)} %param.18) | copy-start | bytes 43204
  81.5 32.6 %copy-start.4 = (f32[50,2048]{0,1:T(8,128)S(1)}, f32[50,2048]{0,1:T(8,128)}, u32[]{:S(2)}) copy-start(f32[50,2048]{0,1:T(8,128)} %copy.38) | copy-start | bytes 1228804
  83.2 10.4 %all-to-all-start = ((f32[4,72,64]{1,2,0:T(8,128)}), f32[4,72,64]{1,2,0:T(8,128)}, u32[]{:S(2)}, u32[]{:S(2)}) async-start(f32[4,72,64]{1,2,0:T(8,128)} %bitcast.40), calls=%async_computation | async-start | bytes 262144 | tf_op jit(solution)/shard_map/all_to_all | solution.py:159
  93.6 8.8 %all-to-all-start.1 = ((f32[1,72,256]{1,0,2:T(1,128)}), f32[1,72,256]{1,0,2:T(1,128)S(1)}, u32[]{:S(2)}, u32[]{:S(2)}) async-start(f32[1,72,256]{1,0,2:T(1,128)} %bitcast.44), calls=%async_computation.1 | async-start | bytes 262144 | tf_op jit(solution)/shard_map/all_to_all | solution.py:158
  103.9 9.6 %all-to-all-start.2 = ((f32[1,72,256]{1,0,2:T(1,128)}), f32[1,72,256]{1,0,2:T(1,128)S(1)}, u32[]{:S(2)}, u32[]{:S(2)}) async-start(f32[1,72,256]{1,0,2:T(1,128)} %bitcast.48), calls=%async_computation.2 | async-start | bytes 262144 | tf_op jit(solution)/shard_map/all_to_all | solution.py:131
  139.0 28.4 %copy-start.8 = (f32[4,4,72,16]{2,3,1,0:T(8,128)S(1)}, f32[4,4,72,16]{2,3,1,0:T(8,128)}, u32[]{:S(2)}) copy-start(f32[4,4,72,16]{2,3,1,0:T(8,128)} %get-tuple-element.30) | copy-start | bytes 221188
  139.0 28.4 %copy-start.9 = (f32[4,16,72]{2,1,0:T(8,128)S(1)}, f32[4,16,72]{2,1,0:T(8,128)}, u32[]{:S(2)}) copy-start(f32[4,16,72]{2,1,0:T(8,128)} %get-tuple-element.27) | copy-start | bytes 55300
where the time goes:
time: 170 us; the launch traced here: 168 us
  local copies, waits for them, and re-layouts  48 us (28%)
  other arithmetic  39.3 us (23%)
  blocking collectives  24.9 us (15%)
  matrix products  19.5 us (11%)
  waiting for transfers between devices  17.9 us (11%)
  starting transfers between devices  17.3 us (10%)
    add x1, other arithmetic, cloud_step(): moved = cloud_fields + TIME_STEP * (advect + diffuse + spread)  11.3 us
    all_to_all x1, blocking collectives, shards(): lax.all_to_all(lax.all_to_all(slot_order, 'cols', split_axis=2, concat_ax...  8.54 us
    all_to_all x1, blocking collectives, to_block(): lax.all_to_all(values, 'vars', split_axis=0, concat_axis=2, tiled=True)  8.43 us
    all_to_all x1, blocking collectives, shards(): lax.all_to_all(slot_order, 'cols', split_axis=2, concat_axis=2, tiled=True)  7.89 us
    ppermute x1, starting transfers between devices, padded_2(): lax.ppermute(lax.slice_in_dim(block, 0, width, axis=dim), axis, backward)  6.46 us
    all_to_all x1, waiting for transfers between devices, shards(): lax.all_to_all(outgoing, 'vars', split_axis=0, concat_axis=2, tiled=True)  6.45 us
    all_to_all x1, waiting for transfers between devices, to_owners(): lax.all_to_all(positioned_blocks, 'vars', split_axis=2, concat_axis=0, ti...  6.02 us
    dot_general x4, matrix products, tendency_of(): jnp.einsum('tn,evnl->evtl', target[edge], own_elems, precision=TOP_LEVEL_...  5.92 us
  transfers between devices with their start and end apart: 5, of which 3 were waited for; matrix products, arithmetic and copies ran while one was open for 41% of the time, Pallas kernels for 0%

commit v1 on v0

v1 whole, which is shorter than its diff:
```python
import functools

import jax
import jax.numpy as jnp
import numpy as np
from jax import lax
from jax.experimental import pallas as pl
from jax.experimental.pallas import tpu as pltpu
from jax.sharding import PartitionSpec as P

CCOL = 32
NODES = 16
LANES = 128
ROWS = 8
AXES = ("cols", "vars")
VISCOSITY = 0.01
DRIFT = 0.05
PENALTY = 0.5
TIME_STEP = 0.5
CLOUD_ADVECT = 0.25
CLOUD_DIFFUSE = 0.1
CONDENSE_RATE = 0.3
SATURATION_BASE = 0.5
SATURATION_SLOPE = 0.3
RETAIN = 0.8
EXACT = lax.Precision.HIGHEST
FAR_ROW = 6
ORDER_ROW = 7


def lobatto_derivative():
    points = np.array([-1.0, -1.0 / np.sqrt(5.0), 1.0 / np.sqrt(5.0), 1.0])
    derivative = np.zeros((4, 4))
    for target in range(4):
        for source in range(4):
            if target != source:
                weight_target = np.prod(
                    [points[target] - points[middle] for middle in range(4) if middle != target]
                )
                weight_source = np.prod(
                    [points[source] - points[middle] for middle in range(4) if middle != source]
                )
                derivative[target, source] = weight_target / (
                    weight_source * (points[target] - points[source])
                )
        derivative[target, target] = np.sum(
            [1.0 / (points[target] - points[middle]) for middle in range(4) if middle != target]
        )
    return derivative


def node_weights():
    derivative = lobatto_derivative()
    along_first = np.kron(np.eye(4), derivative)
    along_second = np.kron(derivative, np.eye(4))
    laplace = along_first @ along_first + along_second @ along_second
    edges = np.zeros((4, 4))
    edges[0, :] += 1.0
    edges[3, :] += 1.0
    edges[:, 0] += 1.0
    edges[:, 3] += 1.0
    linear = VISCOSITY * laplace - PENALTY * np.diag(edges.reshape(-1))
    repeat = np.eye(LANES // NODES)
    return np.concatenate(
        [np.kron(repeat, linear.T), np.kron(repeat, -DRIFT * along_first.T)], axis=1
    ).astype(np.float32)


def each(count, body):
    if count <= 16:
        for index in range(count):
            body(index)
    else:
        lax.fori_loop(0, count, lambda index, carry: (body(index), carry)[1], 0)


def lane_ids(rows=ROWS):
    return lax.broadcasted_iota(jnp.int32, (rows, LANES), 1)


def row_ids():
    return lax.broadcasted_iota(jnp.int32, (ROWS, LANES), 0)


def pick(values, lanes):
    return jnp.take_along_axis(values, lanes, axis=1, mode="promise_in_bounds")


def half_turn(values):
    return pltpu.roll(values, LANES // 2, 1)


def split_pair(first, second):
    lower = lane_ids() < LANES // 2
    return (
        jnp.where(lower, first, half_turn(second)),
        jnp.where(lower, half_turn(first), second),
    )


def row_of(values, row):
    return jnp.broadcast_to(values[row : row + 1], (ROWS, LANES))


def pack_kernel(own_ref, nbr_ref, face_ref, order_ref, state_ref, out_ref, scratch, depth, block):
    elements, variables, nodes, levels = state_ref.shape
    used = levels // depth
    half = LANES // 2
    lane = lane_ids()
    own = own_ref[0]
    column = lane % half
    elem = column // nodes
    along_y = (column // 4) % 4
    along_x = column % 4
    upper = lane >= half
    edge = jnp.where(
        upper,
        jnp.where(along_x == 3, 1, jnp.where(along_x == 0, 3, -1)),
        jnp.where(along_y == 0, 0, jnp.where(along_y == 3, 2, -1)),
    )
    along = jnp.where(upper, along_y, along_x)
    place = jnp.where(edge >= 2, 3 - along, along)
    far = jnp.zeros_like(lane)
    face = jnp.zeros_like(lane)
    for e in range(elements):
        for j in range(4):
            here = (elem == e) & (edge == j)
            far = jnp.where(here, nbr_ref[e, j], far)
            face = jnp.where(here, face_ref[e, j], face)
    node = jnp.where(
        face == 0,
        3 - place,
        jnp.where(face == 1, 15 - 4 * place, jnp.where(face == 2, 12 + place, 4 * place)),
    )
    far_col = jnp.where(edge >= 0, nodes * far + node, -1).astype(jnp.float32)

    order = order_ref[...]
    spots = lax.broadcasted_iota(jnp.int32, (block, block), 0)
    marks = (spots == order).astype(jnp.float32).astype(jnp.bfloat16)
    numbers = lax.broadcasted_iota(jnp.int32, (ROWS, block), 1).astype(jnp.float32)
    scratch[0] = jnp.broadcast_to(order, (ROWS, block)).astype(jnp.float32)
    scratch[1] = lax.dot_general(
        numbers.astype(jnp.bfloat16),
        marks,
        (((1,), (1,)), ((), ())),
        preferred_element_type=jnp.float32,
    )
    begin = pl.multiple_of((own // 2) * LANES, LANES)
    order_part = scratch[0, :, pl.ds(begin, LANES)]
    place_part = scratch[1, :, pl.ds(begin, LANES)]
    odd = own % 2 == 1
    order_part = jnp.where(odd, half_turn(order_part), order_part)
    place_part = jnp.where(odd, place_part, half_turn(place_part))
    indices = jnp.where(upper, place_part, order_part)

    out_ref[...] = jnp.zeros_like(out_ref)
    slots = out_ref.shape[0] // ROWS
    for first in range(0, slots, ROWS):
        out_ref[pl.ds(ROWS * first + FAR_ROW, ROWS, stride=ROWS), :] = far_col
        out_ref[pl.ds(ROWS * first + ORDER_ROW, ROWS, stride=ROWS), :] = indices
    for pair in range(variables // 2):
        fields = jnp.concatenate(
            [
                state_ref[:, pair].reshape(elements * nodes, levels),
                state_ref[:, variables // 2 + pair].reshape(elements * nodes, levels),
            ],
            axis=0,
        )
        by_level = fields.T
        for part in range(depth):
            for first in range(0, used, ROWS):
                begin = used * part + first
                out_ref[pl.ds(ROWS * first + depth * pair + part, ROWS, stride=ROWS), :] = (
                    by_level[begin : begin + ROWS]
                )


def tendency_kernel(got_ref, weight_ref, out_ref, partial_ref, field, linear, tend, depth, share):
    tiles = field.shape[0]
    block = LANES * 2
    tiles_block = block // LANES
    col_count = block // share
    lane = lane_ids()
    row = row_ids()
    lower = lane < LANES // 2

    def unpack(q):
        low, high = split_pair(got_ref[2 * q], got_ref[2 * q + 1])
        field[q, 0] = low
        field[q, 1] = high

    each(tiles, unpack)

    step = min(tiles, 16)

    def multiply(chunk):
        fields = field[pl.ds(chunk * step, step)].reshape(step * 2 * ROWS, LANES)
        result = jnp.dot(fields, weight_ref[...], precision=EXACT)
        linear[pl.ds(chunk * step, step)] = result.reshape(step, 2, ROWS, 2 * LANES)

    each(tiles // step, multiply)

    def advance(q):
        before = (q + tiles - 1) % tiles
        after = (q + 1) % tiles
        high = field[q, 1]
        wind = jnp.where(row < depth, pltpu.roll(high, ROWS - depth, 0), high)
        sums = [jnp.zeros((ROWS, LANES), jnp.float32)] * 2
        for side in range(2):
            far = row_of(field[q, side], FAR_ROW).astype(jnp.int32)
            spot = jnp.maximum(far, 0) % LANES
            inside = far // LANES == q
            for part in range(2):
                beside = jnp.where(lower, field[after, part], field[before, part])
                value = jnp.where(inside, pick(field[q, part], spot), pick(beside, spot))
                sums[part] = sums[part] + jnp.where(far >= 0, value, 0.0)
        for part in range(2):
            own = field[q, part]
            result = (
                linear[q, part, :, :LANES]
                + wind * linear[q, part, :, LANES:]
                + PENALTY * sums[part]
            )
            tend[q, part] = result
            partial_ref[q, part] = jnp.where(row < FAR_ROW, own + TIME_STEP * result, own)

    each(tiles, advance)

    def arrange(p):
        col = p // tiles_block
        order = row_of(field[p, 0], ORDER_ROW).astype(jnp.int32)
        owner = order // share
        spot = (share * col) % LANES + order % share
        base = (share * col) // LANES
        parts = [jnp.zeros((ROWS, LANES), jnp.float32)] * 2
        for k in range(col_count):
            for part in range(2):
                source = tend[tiles_block * k + base, part]
                parts[part] = jnp.where(owner == k, pick(source, spot), parts[part])
        first, second = split_pair(parts[0], parts[1])
        out_ref[2 * p] = first
        out_ref[2 * p + 1] = second

    each(tiles, arrange)


def cloud_kernel(
    got_ref, down_ref, up_ref, cloud_ref, next_ref, out_ref, forced, pooled, depth, levels
):
    clev, variables, width = cloud_ref.shape
    used = levels // depth
    lane = lane_ids()
    row = row_ids()
    half = LANES // 2
    lower = lane < half
    rows = clev * variables
    for pair in range(2):
        fields = jnp.concatenate(
            [
                got_ref[pl.ds(ROWS * first + depth * pair + part, ROWS, stride=ROWS), :]
                for part in range(depth)
                for first in range(0, used, ROWS)
            ],
            axis=0,
        )
        forcing = TIME_STEP * jnp.dot(down_ref[...], fields, precision=EXACT)
        turned = half_turn(forcing)
        for first in range(0, clev, ROWS):
            count = min(ROWS, clev - first)
            forced[pl.ds(variables * first + pair, count, stride=variables), :] = forcing[
                first : first + count
            ]
            forced[pl.ds(variables * first + 2 + pair, count, stride=variables), :] = turned[
                first : first + count
            ]
    pooled[...] = jnp.zeros_like(pooled)
    within = lane % CCOL
    var = row % variables
    wind_row = (row // variables) * variables + 3
    lead_row = (row // variables) * variables
    keep = jnp.where(var == 2, RETAIN, 1.0).astype(jnp.float32)
    sign = jnp.where(var == 1, -1.0, jnp.where(var == 3, 0.0, 1.0)).astype(jnp.float32)
    first_half = row < variables
    pool_lane = lax.broadcasted_iota(jnp.int32, (LANES, LANES), 1) % half
    pool_row = lax.broadcasted_iota(jnp.int32, (LANES, LANES), 0) // CCOL
    pairs = clev // 2

    def tile(t, carry):
        begin = pl.multiple_of(t * LANES, LANES)

        def load(a):
            return cloud_ref[2 * a : 2 * a + 2, :, pl.ds(begin, LANES)].reshape(ROWS, LANES)

        spread = (LANES // CCOL) * t + lane // CCOL
        zero = jnp.zeros((ROWS, LANES), jnp.float32)
        turned_before = zero
        now = load(0)
        turned = pltpu.roll(now, variables, 0)
        changes = []
        for a in range(pairs):
            following = load(a + 1) if a + 1 < pairs else zero
            turned_after = pltpu.roll(following, variables, 0) if a + 1 < pairs else zero
            above = jnp.where(first_half, turned, turned_after)
            below = jnp.where(first_half, turned_before, turned)
            ahead = jnp.where(
                within == CCOL - 1, pltpu.roll(now, CCOL - 1, 1), pltpu.roll(now, LANES - 1, 1)
            )
            behind = jnp.where(
                within == 0, pltpu.roll(now, LANES - CCOL + 1, 1), pltpu.roll(now, 1, 1)
            )
            wind = jnp.take_along_axis(now, wind_row, axis=0, mode="promise_in_bounds")
            advect = (-CLOUD_ADVECT * TIME_STEP) * wind * (ahead - behind)
            diffuse = (CLOUD_DIFFUSE * TIME_STEP) * (above - 2.0 * now + below)
            push = pick(forced[ROWS * a : ROWS * a + ROWS, :], spread)
            moved = now + (advect + diffuse + push)
            excess = pltpu.roll(moved, ROWS - 1, 0) - SATURATION_BASE * jnp.exp(
                SATURATION_SLOPE * moved
            )
            soft = jnp.maximum(excess, 0.0) + jnp.log1p(jnp.exp(-jnp.abs(excess)))
            condensed = CONDENSE_RATE * jnp.take_along_axis(
                soft, lead_row, axis=0, mode="promise_in_bounds"
            )
            updated = keep * moved + sign * condensed
            next_ref[2 * a : 2 * a + 2, :, pl.ds(begin, LANES)] = updated.reshape(
                2, variables, LANES
            )
            changes.append(updated - now)
            turned_before, turned, now = turned, turned_after, following
        change = jnp.concatenate(changes, axis=0)
        pool = jnp.where(
            pool_lane == (LANES // CCOL) * t + pool_row, 1.0 / (CCOL * TIME_STEP), 0.0
        ).astype(jnp.float32)
        pooled[...] += jnp.dot(change, pool, precision=EXACT)
        return carry

    lax.fori_loop(0, width // LANES, tile, 0)
    for pair in range(2):
        mean = jnp.where(
            lane_ids(clev) < half,
            pooled[pl.ds(pair, clev, stride=variables), :],
            pooled[pl.ds(2 + pair, clev, stride=variables), :],
        )
        feedback = jnp.dot(up_ref[...], mean, precision=EXACT)
        for part in range(depth):
            for first in range(0, used, ROWS):
                begin = used * part + first
                out_ref[pl.ds(ROWS * first + depth * pair + part, ROWS, stride=ROWS), :] = (
                    feedback[begin : begin + ROWS]
                )


def update_kernel(got_ref, partial_ref, out_ref, field, share):
    tiles = field.shape[0]
    block = LANES * 2
    tiles_block = block // LANES
    lane = lane_ids()
    groups = LANES // share
    group = lane // share
    inner = lane % share

    def unpack(p):
        low, high = split_pair(got_ref[2 * p], got_ref[2 * p + 1])
        field[p, 0] = low
        field[p, 1] = high

    each(tiles, unpack)

    def collect(q):
        k = q // tiles_block
        start = (LANES * (q % tiles_block)) // share
        offset = share * k
        place = jnp.zeros((ROWS, LANES), jnp.float32)
        for g in range(groups):
            source = row_of(partial_ref[tiles_block * (start + g) + offset // LANES, 1], ORDER_ROW)
            place = jnp.where(group == g, pick(source, offset % LANES + inner), place)
        place = place.astype(jnp.int32)
        spot = place % LANES
        parts = [jnp.zeros((ROWS, LANES), jnp.float32)] * 2
        for g in range(groups):
            for piece in range(tiles_block):
                chosen = (group == g) & (place // LANES == piece)
                for part in range(2):
                    source = field[tiles_block * (start + g) + piece, part]
                    parts[part] = jnp.where(chosen, pick(source, spot), parts[part])
        low = partial_ref[q, 0] + TIME_STEP * parts[0]
        high = partial_ref[q, 1] + TIME_STEP * parts[1]
        first, second = split_pair(low, high)
        out_ref[2 * q] = first
        out_ref[2 * q + 1] = second

    each(tiles, collect)


def unpack_kernel(got_ref, state_ref, depth):
    elements, variables, nodes, levels = state_ref.shape
    used = levels // depth
    for pair in range(variables // 2):
        by_level = jnp.concatenate(
            [
                got_ref[pl.ds(ROWS * first + depth * pair + part, ROWS, stride=ROWS), :]
                for part in range(depth)
                for first in range(0, used, ROWS)
            ],
            axis=0,
        )
        fields = by_level.T.reshape(2, elements, nodes, levels)
        state_ref[:, pair] = fields[0]
        state_ref[:, variables // 2 + pair] = fields[1]


def kernel_call(body, name, results, scratch, *operands, spaces=None):
    vmem = pl.BlockSpec(memory_space=pltpu.VMEM)
    smem = pl.BlockSpec(memory_space=pltpu.SMEM)
    return pl.pallas_call(
        body,
        name=name,
        out_shape=results,
        in_specs=[smem if spaces and n in spaces else vmem for n in range(len(operands))],
        out_specs=jax.tree.map(lambda _: vmem, results),
        scratch_shapes=scratch,
    )(*operands)


def exchange(slots):
    return lax.all_to_all(slots, AXES, split_axis=0, concat_axis=0, tiled=True)


def shards(
    model_state,
    cloud_state,
    neighbor,
    facing_edge,
    column_order,
    model_to_cloud_levels,
    cloud_to_model_levels,
):
    elements, variables, nodes, levels = model_state.shape
    clev, width = cloud_state.shape[1:]
    devices = lax.axis_size(AXES)
    block = column_order.shape[1]
    share = block // lax.axis_size("cols")
    depth = -(-levels // devices)
    assert variables == 4 and nodes == NODES and 2 * elements * nodes == LANES
    assert 2 * depth <= FAR_ROW and levels % (ROWS * depth) == 0 and block == 2 * LANES
    tiles = devices // 2
    f32 = jnp.float32
    shape = jax.ShapeDtypeStruct
    flat = shape((devices * ROWS, LANES), f32)
    slots = shape((devices, ROWS, LANES), f32)
    pairs = shape((tiles, 2, ROWS, LANES), f32)
    own = lax.axis_index("vars").astype(jnp.int32).reshape(1)

    packed = kernel_call(
        functools.partial(pack_kernel, depth=depth, block=block),
        "pack_state",
        flat,
        [pltpu.VMEM((2, ROWS, block), f32)],
        own,
        neighbor,
        facing_edge,
        column_order,
        model_state,
        spaces=(0, 1, 2),
    )
    by_level = exchange(packed.reshape(slots.shape))
    arranged, partial = kernel_call(
        functools.partial(tendency_kernel, depth=depth, share=share),
        "tendency",
        (slots, pairs),
        [
            pltpu.VMEM(pairs.shape, f32),
            pltpu.VMEM((tiles, 2, ROWS, 2 * LANES), f32),
            pltpu.VMEM(pairs.shape, f32),
        ],
        by_level,
        jnp.asarray(node_weights()),
    )
    by_column = exchange(arranged)
    cloud_next, fed = kernel_call(
        functools.partial(cloud_kernel, depth=depth, levels=levels),
        "cloud",
        (shape((clev, variables, width), f32), flat),
        [
            pltpu.VMEM((clev * variables, LANES), f32),
            pltpu.VMEM((clev * variables, LANES), f32),
        ],
        by_column.reshape(flat.shape),
        model_to_cloud_levels,
        cloud_to_model_levels,
        jnp.transpose(cloud_state, (1, 0, 2)),
    )
    fed_level = exchange(fed.reshape(slots.shape))
    advanced = kernel_call(
        functools.partial(update_kernel, share=share),
        "update",
        slots,
        [pltpu.VMEM(pairs.shape, f32)],
        fed_level,
        partial,
    )
    home = exchange(advanced)
    model_next = kernel_call(
        functools.partial(unpack_kernel, depth=depth),
        "unpack_state",
        shape(model_state.shape, f32),
        [],
        home.reshape(flat.shape),
    )
    return (model_next, jnp.transpose(cloud_next, (1, 0, 2)))


def solution(mesh):
    placed = (
        P(AXES, None, None, None),
        P(None, None, AXES),
        P(AXES, None),
        P(AXES, None),
        P("cols", None),
        P(),
        P(),
    )
    return jax.shard_map(
        shards,
        mesh=mesh,
        in_specs=placed,
        out_specs=(P(AXES, None, None, None), P(None, None, AXES)),
        check_vma=False,
    )
```

time: 170 us -> 73.2 us (0.43)
  local copies, waits for them, and re-layouts: 48 us -> 2.1 us
  other arithmetic: 39.3 us -> 0 us
  Pallas kernels: 0 us -> 21.4 us
  matrix products: 19.5 us -> 0 us
  starting transfers between devices: 17.3 us -> 2.58 us
  blocking collectives: 24.9 us -> 39.1 us
  waiting for transfers between devices: 17.9 us -> 6.93 us
    pallas_call x0 -> x5, Pallas kernels: none -> 21.4 us  [kernel_call(): pl.pallas_call(body, name=name, out_shape=results, in_specs=[smem if spac...]
    dot_general x21 -> x0, matrix products: 19.5 us -> none  [the longest x4 5.92 us: tendency_of(): jnp.einsum('tn,evnl->evtl', target[edge], own_elems, precision=TOP_LEVEL_...]
    concatenate x5 -> x0, local copies, waits for them, and re-layouts: 17.6 us -> none  [the longest x1 4.54 us: cloud_step(): jnp.roll(cloud_fields, -(CCOL - 1), axis=2)]
    add x3 -> x0, other arithmetic: 14.3 us -> none  [the longest x1 11.3 us: cloud_step(): moved = cloud_fields + TIME_STEP * (advect + diffuse + spread)]
    all_to_all x3, blocking collectives: 24.9 us -> 39.1 us  [exchange(): return lax.all_to_all(slots, AXES, split_axis=0, concat_axis=0, tiled=True)]
    slice x8 -> x0, local copies, waits for them, and re-layouts: 13.5 us -> none  [the longest x2 4.46 us: cloud_step(): jnp.roll(cloud_fields, -1, axis=2)]
    all_to_all x3 -> x1, waiting for transfers between devices: 17.9 us -> 6.93 us  [exchange(): return lax.all_to_all(slots, AXES, split_axis=0, concat_axis=0, tiled=True)]
    concatenate x2 -> x0, other arithmetic: 9.01 us -> none  [the longest x1 4.72 us: cloud_step(): jnp.roll(cloud_fields, -1, axis=2)]
  transfers between devices with their start and end apart: 5 -> 1, of which waited for: 3 -> 1; matrix products, arithmetic and copies ran while one was open for 41% -> 2% of each run, Pallas kernels for 0% -> 0%
where the time goes in v1:
time: 73.2 us; the launch traced here: 72.7 us
  blocking collectives  39.1 us (53%)
  Pallas kernels  21.4 us (29%)
  waiting for transfers between devices  6.93 us (9%)
  starting transfers between devices  2.58 us (4%)
  local copies, waits for them, and re-layouts  2.1 us (3%)
    all_to_all x3, blocking collectives, exchange(): return lax.all_to_all(slots, AXES, split_axis=0, concat_axis=0, tiled=True)  39.1 us
    pallas_call x5, Pallas kernels, kernel_call(): pl.pallas_call(body, name=name, out_shape=results, in_specs=[smem if spac...  21.4 us
    all_to_all x1, waiting for transfers between devices, exchange(): return lax.all_to_all(slots, AXES, split_axis=0, concat_axis=0, tiled=True)  6.93 us
    all_to_all x1, starting transfers between devices, exchange(): return lax.all_to_all(slots, AXES, split_axis=0, concat_axis=0, tiled=True)  2.58 us
    unnamed x3, local copies, waits for them, and re-layouts  2.1 us
  transfers between devices with their start and end apart: 1, of which 1 were waited for; matrix products, arithmetic and copies ran while one was open for 2% of the time, Pallas kernels for 0%

profile of v1, /device:TPU:0, one launch (start us, length us, event | category | flops | bytes accessed | tf_op | source)
XLA Modules:
  0.0 72.7 jit_solution(18417390059666409385)
XLA Ops:
  0.6 1.9 %pack_state.1 = f32[256,128]{1,0:T(8,128)} custom-call(s32[1]{0:T(128)} %bitcast.own_ref, s32[4,4]{1,0:T(4,128)} %nbr_ref.1, s32[4,4]{1,0:T(4,128)} %face_ref.1, s32[1,256]{1,0:T(1,128)} %order_ref.1, f32[4,4,16,72]{3,2,1,0:T(8,128)} %state_ref.1), custom_call_target="tpu_custom_call" | custom-call | tf_op jit(solution)/shard_map/pack_state/pallas_call | solution.py:414
  2.5 15.8 %all_to_all.20.got_ref = f32[32,8,128]{2,1,0:T(8,128)} all-to-all(f32[32,8,128]{2,1,0:T(8,128)} %bitcast.9), channel_id=1, replica_groups=mesh['cols'=8,'vars'=4] {'cols','vars'}, dimensions={0} | all-to-all | bytes 262144 | tf_op jit(solution)/shard_map/all_to_all | solution.py:425
  18.3 2.7 %tendency.1 = (f32[32,8,128]{2,1,0:T(8,128)}, f32[16,2,8,128]{3,2,1,0:T(8,128)}) custom-call(f32[32,8,128]{2,1,0:T(8,128)} %all_to_all.20.got_ref, f32[128,256]{1,0:T(8,128)} %constant.6.clone.weight_ref), custom_call_target="tpu_custom_call" | custom-call | tf_op jit(solution)/shard_map/tendency/pallas_call | solution.py:414
  21.1 2.6 %all-to-all-start.1 = ((f32[32,8,128]{2,1,0:T(8,128)}), f32[32,8,128]{2,1,0:T(8,128)S(1)}, u32[]{:S(2)}, u32[]{:S(2)}) async-start(f32[32,8,128]{2,1,0:T(8,128)} %get-tuple-element.6), calls=%async_computation.1 | async-start | bytes 262144 | tf_op jit(solution)/shard_map/all_to_all | solution.py:425
  23.6 1.4 %copy.10.up_ref = f32[72,50]{1,0:T(8,128)} copy(f32[72,50]{0,1:T(8,128)} %param.14) | data formatting | bytes 28800 | tf_op args[6]
  25.1 6.9 %all-to-all-done.1 = f32[32,8,128]{2,1,0:T(8,128)S(1)} async-done(((f32[32,8,128]{2,1,0:T(8,128)}), f32[32,8,128]{2,1,0:T(8,128)S(1)}, u32[]{:S(2)}, u32[]{:S(2)}) %all-to-all-start.1) | async-done | bytes 131104 | tf_op jit(solution)/shard_map/all_to_all | solution.py:425
  32.0 0.0 copy-start
  32.0 0.7 copy-done
  32.7 11.3 %cloud.1 = (f32[50,4,2048]{2,1,0:T(4,128)}, f32[256,128]{1,0:T(8,128)}) custom-call(f32[256,128]{1,0:T(8,128)} %bitcast.8, f32[50,72]{1,0:T(8,128)} %down_ref.1, f32[72,50]{1,0:T(8,128)} %copy.10.up_ref, f32[50,4,2048]{2,1,0:T(4,128)} %bitcast.7), custom_call_target="tpu_custom_call" | custom-call | tf_op jit(solution)/shard_map/cloud/pallas_call | solution.py:414
  43.9 11.6 %all_to_all.21.got_ref = f32[32,8,128]{2,1,0:T(8,128)} all-to-all(f32[32,8,128]{2,1,0:T(8,128)} %bitcast.11), channel_id=1, replica_groups=mesh['cols'=8,'vars'=4] {'cols','vars'}, dimensions={0} | all-to-all | bytes 262144 | tf_op jit(solution)/shard_map/all_to_all | solution.py:425
  55.6 3.8 %update.1 = f32[32,8,128]{2,1,0:T(8,128)} custom-call(f32[32,8,128]{2,1,0:T(8,128)} %all_to_all.21.got_ref, f32[16,2,8,128]{3,2,1,0:T(8,128)} %get-tuple-element.8.partial_ref), custom_call_target="tpu_custom_call" | custom-call | tf_op jit(solution)/shard_map/update/pallas_call | solution.py:414
  59.4 11.6 %all_to_all.22 = f32[32,8,128]{2,1,0:T(8,128)} all-to-all(f32[32,8,128]{2,1,0:T(8,128)} %update.1), channel_id=1, replica_groups=mesh['cols'=8,'vars'=4] {'cols','vars'}, dimensions={0} | all-to-all | bytes 262144 | tf_op jit(solution)/shard_map/all_to_all | solution.py:425
  71.1 1.7 %unpack_state.1 = f32[4,4,16,72]{3,2,1,0:T(8,128)} custom-call(f32[256,128]{1,0:T(8,128)} %bitcast.10), custom_call_target="tpu_custom_call" | custom-call | tf_op jit(solution)/shard_map/unpack_state/pallas_call | solution.py:414
Async XLA Ops:
  21.1 11.0 %all-to-all-start.1 = ((f32[32,8,128]{2,1,0:T(8,128)}), f32[32,8,128]{2,1,0:T(8,128)S(1)}, u32[]{:S(2)}, u32[]{:S(2)}) async-start(f32[32,8,128]{2,1,0:T(8,128)} %get-tuple-element.6), calls=%async_computation.1 | async-start | bytes 262144 | tf_op jit(solution)/shard_map/all_to_all | solution.py:425
  32.0 0.7 copy-start

commit v2 on v1

--- a/solution.py
+++ b/solution.py
@@ -24,6 +24,7 @@
 SATURATION_SLOPE = 0.3
 RETAIN = 0.8
 EXACT = lax.Precision.HIGHEST
+KERNEL_VMEM = 16 * 2**20
 FAR_ROW = 6
 ORDER_ROW = 7
 
@@ -102,12 +103,42 @@
     return jnp.broadcast_to(values[row : row + 1], (ROWS, LANES))
 
 
-def pack_kernel(own_ref, nbr_ref, face_ref, order_ref, state_ref, out_ref, scratch, depth, block):
+def pack_kernel(
+    nbr_hbm,
+    face_hbm,
+    order_hbm,
+    state_hbm,
+    weight_hbm,
+    out_ref,
+    weight_ref,
+    nbr_ref,
+    face_ref,
+    order_ref,
+    state_ref,
+    scratch,
+    sems,
+    depth,
+    block,
+):
+    copies = [
+        pltpu.make_async_copy(source, target, sems.at[n])
+        for n, (source, target) in enumerate(
+            (
+                (nbr_hbm, nbr_ref),
+                (face_hbm, face_ref),
+                (order_hbm, order_ref),
+                (state_hbm, state_ref),
+                (weight_hbm, weight_ref),
+            )
+        )
+    ]
+    for copy in copies:
+        copy.start()
     elements, variables, nodes, levels = state_ref.shape
     used = levels // depth
     half = LANES // 2
     lane = lane_ids()
-    own = own_ref[0]
+    own = lax.axis_index("vars")
     column = lane % half
     elem = column // nodes
     along_y = (column // 4) % 4
@@ -120,6 +151,9 @@
     )
     along = jnp.where(upper, along_y, along_x)
     place = jnp.where(edge >= 2, 3 - along, along)
+    out_ref[...] = jnp.zeros_like(out_ref)
+    copies[0].wait()
+    copies[1].wait()
     far = jnp.zeros_like(lane)
     face = jnp.zeros_like(lane)
     for e in range(elements):
@@ -134,6 +168,7 @@
     )
     far_col = jnp.where(edge >= 0, nodes * far + node, -1).astype(jnp.float32)
 
+    copies[2].wait()
     order = order_ref[...]
     spots = lax.broadcasted_iota(jnp.int32, (block, block), 0)
     marks = (spots == order).astype(jnp.float32).astype(jnp.bfloat16)
@@ -153,11 +188,11 @@
     place_part = jnp.where(odd, place_part, half_turn(place_part))
     indices = jnp.where(upper, place_part, order_part)
 
-    out_ref[...] = jnp.zeros_like(out_ref)
     slots = out_ref.shape[0] // ROWS
     for first in range(0, slots, ROWS):
         out_ref[pl.ds(ROWS * first + FAR_ROW, ROWS, stride=ROWS), :] = far_col
         out_ref[pl.ds(ROWS * first + ORDER_ROW, ROWS, stride=ROWS), :] = indices
+    copies[3].wait()
     for pair in range(variables // 2):
         fields = jnp.concatenate(
             [
@@ -173,6 +208,7 @@
                 out_ref[pl.ds(ROWS * first + depth * pair + part, ROWS, stride=ROWS), :] = (
                     by_level[begin : begin + ROWS]
                 )
+    copies[4].wait()
 
 
 def tendency_kernel(got_ref, weight_ref, out_ref, partial_ref, field, linear, tend, depth, share):
@@ -244,59 +280,67 @@
     each(tiles, arrange)
 
 
-def cloud_kernel(
-    got_ref, down_ref, up_ref, cloud_ref, next_ref, out_ref, forced, pooled, depth, levels
+def in_two(values):
+    high = values.astype(jnp.bfloat16)
+    low = (values - high.astype(jnp.float32)).astype(jnp.bfloat16)
+    return high, low
+
+
+def pool_weights(step, wide):
+    lane = lax.broadcasted_iota(jnp.int32, (wide, LANES), 1) % (LANES // 2)
+    owner = lax.broadcasted_iota(jnp.int32, (wide, LANES), 0) // CCOL
+    mean = 1.0 / (CCOL * TIME_STEP)
+    return jnp.where(lane == (wide // CCOL) * step + owner, mean, 0.0).astype(jnp.bfloat16)
+
+
+def pooled_sum(tiles, step):
+    rows = ROWS * len(tiles[0])
+    joined = jnp.concatenate([jnp.concatenate(tile, axis=0) for tile in tiles], axis=1)
+    high, low = in_two(joined)
+    both = jnp.concatenate([high, low], axis=0)
+    weights = pool_weights(step, LANES * len(tiles))
+    result = jnp.dot(both, weights, preferred_element_type=jnp.float32)
+    return result[:rows] + result[rows:]
+
+
+def settle_kernel(
+    cloud_hbm, down_hbm, up_hbm, base_ref, mean_ref, down_ref, up_ref, cloud_ref, sems, wide
 ):
     clev, variables, width = cloud_ref.shape
-    used = levels // depth
+    steps = width // (LANES * wide)
+    span = LANES * wide
+    small = [
+        pltpu.make_async_copy(down_hbm, down_ref, sems.at[steps]),
+        pltpu.make_async_copy(up_hbm, up_ref, sems.at[steps + 1]),
+    ]
+
+    def fetch(n):
+        here = pl.ds(pl.multiple_of(n * span, span), span)
+        return pltpu.make_async_copy(
+            cloud_hbm.at[:, :, here], cloud_ref.at[:, :, here], sems.at[n]
+        )
+
+    for n in range(steps):
+        fetch(n).start()
+    for copy in small:
+        copy.start()
+    mean_ref[...] = jnp.zeros_like(mean_ref)
     lane = lane_ids()
     row = row_ids()
-    half = LANES // 2
-    lower = lane < half
-    rows = clev * variables
-    for pair in range(2):
-        fields = jnp.concatenate(
-            [
-                got_ref[pl.ds(ROWS * first + depth * pair + part, ROWS, stride=ROWS), :]
-                for part in range(depth)
-                for first in range(0, used, ROWS)
-            ],
-            axis=0,
-        )
-        forcing = TIME_STEP * jnp.dot(down_ref[...], fields, precision=EXACT)
-        turned = half_turn(forcing)
-        for first in range(0, clev, ROWS):
-            count = min(ROWS, clev - first)
-            forced[pl.ds(variables * first + pair, count, stride=variables), :] = forcing[
-                first : first + count
-            ]
-            forced[pl.ds(variables * first + 2 + pair, count, stride=variables), :] = turned[
-                first : first + count
-            ]
-    pooled[...] = jnp.zeros_like(pooled)
     within = lane % CCOL
-    var = row % variables
     wind_row = (row // variables) * variables + 3
-    lead_row = (row // variables) * variables
-    keep = jnp.where(var == 2, RETAIN, 1.0).astype(jnp.float32)
-    sign = jnp.where(var == 1, -1.0, jnp.where(var == 3, 0.0, 1.0)).astype(jnp.float32)
     first_half = row < variables
-    pool_lane = lax.broadcasted_iota(jnp.int32, (LANES, LANES), 1) % half
-    pool_row = lax.broadcasted_iota(jnp.int32, (LANES, LANES), 0) // CCOL
     pairs = clev // 2
-
-    def tile(t, carry):
-        begin = pl.multiple_of(t * LANES, LANES)
-
+    zero = jnp.zeros((ROWS, LANES), jnp.float32)
+
+    def tile(begin):
         def load(a):
             return cloud_ref[2 * a : 2 * a + 2, :, pl.ds(begin, LANES)].reshape(ROWS, LANES)
 
-        spread = (LANES // CCOL) * t + lane // CCOL
-        zero = jnp.zeros((ROWS, LANES), jnp.float32)
         turned_before = zero
         now = load(0)
         turned = pltpu.roll(now, variables, 0)
-        changes = []
+        seen = []
         for a in range(pairs):
             following = load(a + 1) if a + 1 < pairs else zero
             turned_after = pltpu.roll(following, variables, 0) if a + 1 < pairs else zero
@@ -311,42 +355,130 @@
             wind = jnp.take_along_axis(now, wind_row, axis=0, mode="promise_in_bounds")
             advect = (-CLOUD_ADVECT * TIME_STEP) * wind * (ahead - behind)
             diffuse = (CLOUD_DIFFUSE * TIME_STEP) * (above - 2.0 * now + below)
+            base_ref[ROWS * a : ROWS * a + ROWS, pl.ds(begin, LANES)] = now + (advect + diffuse)
+            seen.append(now)
+            turned_before, turned, now = turned, turned_after, following
+        return seen
+
+    def advance(step, carry):
+        fetch(step).wait()
+        tiles = [tile(pl.multiple_of(step * span + LANES * n, LANES)) for n in range(wide)]
+        mean_ref[...] += pooled_sum(tiles, step)
+        return carry
+
+    lax.fori_loop(0, steps, advance, 0)
+    for copy in small:
+        copy.wait()
+
+
+def cloud_kernel(
+    got_ref,
+    base_ref,
+    mean_ref,
+    down_ref,
+    up_ref,
+    next_hbm,
+    out_ref,
+    forced,
+    pooled,
+    next_ref,
+    sem,
+    depth,
+    levels,
+    wide,
+):
+    clev, variables, width = next_ref.shape
+    steps = width // (LANES * wide)
+    span = LANES * wide
+    used = levels // depth
+    lane = lane_ids()
+    row = row_ids()
+    half = LANES // 2
+    fields = jnp.concatenate(
+        [
+            jnp.concatenate(
+                [
+                    got_ref[pl.ds(ROWS * first + depth * pair + part, ROWS, stride=ROWS), :]
+                    for part in range(depth)
+                    for first in range(0, used, ROWS)
+                ],
+                axis=0,
+            )
+            for pair in range(2)
+        ],
+        axis=1,
+    )
+    forcing = TIME_STEP * jnp.dot(down_ref[...], fields, precision=EXACT)
+    for pair in range(2):
+        straight = forcing[:, LANES * pair : LANES * pair + LANES]
+        turned = half_turn(straight)
+        for first in range(0, clev, ROWS):
+            count = min(ROWS, clev - first)
+            for shift, values in ((0, straight), (2, turned)):
+                forced[
+                    pl.ds(variables * first + shift + pair, count, stride=variables), :
+                ] = values[first : first + count]
+    pooled[...] = -mean_ref[...]
+    var = row % variables
+    lead_row = (row // variables) * variables
+    keep = jnp.where(var == 2, RETAIN, 1.0).astype(jnp.float32)
+    sign = jnp.where(var == 1, -1.0, jnp.where(var == 3, 0.0, 1.0)).astype(jnp.float32)
+    sign = CONDENSE_RATE * sign
+    pairs = clev // 2
+
+    def tile(begin, index):
+        spread = (LANES // CCOL) * index + lane // CCOL
+        results = []
+        for a in range(pairs):
             push = pick(forced[ROWS * a : ROWS * a + ROWS, :], spread)
-            moved = now + (advect + diffuse + push)
+            moved = base_ref[ROWS * a : ROWS * a + ROWS, pl.ds(begin, LANES)] + push
             excess = pltpu.roll(moved, ROWS - 1, 0) - SATURATION_BASE * jnp.exp(
                 SATURATION_SLOPE * moved
             )
-            soft = jnp.maximum(excess, 0.0) + jnp.log1p(jnp.exp(-jnp.abs(excess)))
-            condensed = CONDENSE_RATE * jnp.take_along_axis(
-                soft, lead_row, axis=0, mode="promise_in_bounds"
-            )
+            soft = jnp.maximum(excess, 0.0) + jnp.log(1.0 + jnp.exp(-jnp.abs(excess)))
+            condensed = jnp.take_along_axis(soft, lead_row, axis=0, mode="promise_in_bounds")
             updated = keep * moved + sign * condensed
             next_ref[2 * a : 2 * a + 2, :, pl.ds(begin, LANES)] = updated.reshape(
                 2, variables, LANES
             )
-            changes.append(updated - now)
-            turned_before, turned, now = turned, turned_after, following
-        change = jnp.concatenate(changes, axis=0)
-        pool = jnp.where(
-            pool_lane == (LANES // CCOL) * t + pool_row, 1.0 / (CCOL * TIME_STEP), 0.0
-        ).astype(jnp.float32)
-        pooled[...] += jnp.dot(change, pool, precision=EXACT)
+            results.append(updated)
+        return results
+
+    def store(step):
+        here = pl.ds(pl.multiple_of(step * span, span), span)
+        return pltpu.make_async_copy(next_ref.at[:, :, here], next_hbm.at[:, :, here], sem)
+
+    def advance(step, carry):
+        tiles = [
+            tile(pl.multiple_of(step * span + LANES * n, LANES), wide * step + n)
+            for n in range(wide)
+        ]
+        store(step).start()
+        pooled[...] += pooled_sum(tiles, step)
         return carry
 
-    lax.fori_loop(0, width // LANES, tile, 0)
+    lax.fori_loop(0, steps, advance, 0)
+    lower = lane_ids(clev) < half
+    mean = jnp.concatenate(
+        [
+            jnp.where(
+                lower,
+                pooled[pl.ds(pair, clev, stride=variables), :],
+                pooled[pl.ds(2 + pair, clev, stride=variables), :],
+            )
+            for pair in range(2)
+        ],
+        axis=1,
+    )
+    feedback = lax.dot_general(up_ref[...], mean, (((0,), (0,)), ((), ())), precision=EXACT)
     for pair in range(2):
-        mean = jnp.where(
-            lane_ids(clev) < half,
-            pooled[pl.ds(pair, clev, stride=variables), :],
-            pooled[pl.ds(2 + pair, clev, stride=variables), :],
-        )
-        feedback = jnp.dot(up_ref[...], mean, precision=EXACT)
         for part in range(depth):
             for first in range(0, used, ROWS):
                 begin = used * part + first
                 out_ref[pl.ds(ROWS * first + depth * pair + part, ROWS, stride=ROWS), :] = (
-                    feedback[begin : begin + ROWS]
+                    feedback[begin : begin + ROWS, LANES * pair : LANES * pair + LANES]
                 )
+    pltpu.make_async_copy(next_ref, next_hbm, sem).wait()
 
 
 def update_kernel(got_ref, partial_ref, out_ref, field, share):
@@ -408,16 +540,21 @@
         state_ref[:, variables // 2 + pair] = fields[1]
 
 
-def kernel_call(body, name, results, scratch, *operands, spaces=None):
-    vmem = pl.BlockSpec(memory_space=pltpu.VMEM)
-    smem = pl.BlockSpec(memory_space=pltpu.SMEM)
+def kernel_call(body, name, results, scratch, *operands, hbm_in=(), hbm_out=(), cost=None):
+    spec = {True: pl.BlockSpec(memory_space=pltpu.HBM), False: pl.BlockSpec(memory_space=pltpu.VMEM)}
+    operands = [
+        pltpu.with_memory_space_constraint(value, pltpu.HBM) if n in hbm_in else value
+        for n, value in enumerate(operands)
+    ]
     return pl.pallas_call(
         body,
         name=name,
         out_shape=results,
-        in_specs=[smem if spaces and n in spaces else vmem for n in range(len(operands))],
-        out_specs=jax.tree.map(lambda _: vmem, results),
+        in_specs=[spec[n in hbm_in] for n in range(len(operands))],
+        out_specs=tuple(spec[n in hbm_out] for n in range(len(results))),
         scratch_shapes=scratch,
+        cost_estimate=cost,
+        compiler_params=pltpu.CompilerParams(vmem_limit_bytes=KERNEL_VMEM),
     )(*operands)
 
 
@@ -448,19 +585,28 @@
     flat = shape((devices * ROWS, LANES), f32)
     slots = shape((devices, ROWS, LANES), f32)
     pairs = shape((tiles, 2, ROWS, LANES), f32)
-    own = lax.axis_index("vars").astype(jnp.int32).reshape(1)
-
-    packed = kernel_call(
+    columns = width // LANES
+    wide = 2 if columns % 2 == 0 else 1
+    dma = pltpu.SemaphoreType.DMA
+
+    packed, weights = kernel_call(
         functools.partial(pack_kernel, depth=depth, block=block),
         "pack_state",
-        flat,
-        [pltpu.VMEM((2, ROWS, block), f32)],
-        own,
+        (flat, shape((LANES, 2 * LANES), f32)),
+        [
+            pltpu.SMEM(neighbor.shape, jnp.int32),
+            pltpu.SMEM(facing_edge.shape, jnp.int32),
+            pltpu.VMEM(column_order.shape, jnp.int32),
+            pltpu.VMEM(model_state.shape, f32),
+            pltpu.VMEM((2, ROWS, block), f32),
+            dma((5,)),
+        ],
         neighbor,
         facing_edge,
         column_order,
         model_state,
-        spaces=(0, 1, 2),
+        jnp.asarray(node_weights()),
+        hbm_in=range(5),
     )
     by_level = exchange(packed.reshape(slots.shape))
     arranged, partial = kernel_call(
@@ -473,36 +619,56 @@
             pltpu.VMEM(pairs.shape, f32),
         ],
         by_level,
-        jnp.asarray(node_weights()),
+        weights,
+    )
+    base, mean, down, up = kernel_call(
+        functools.partial(settle_kernel, wide=wide),
+        "settle",
+        (
+            shape((clev * variables, width), f32),
+            shape((clev * variables, LANES), f32),
+            shape((clev, levels), f32),
+            shape((clev, levels), f32),
+        ),
+        [pltpu.VMEM((clev, variables, width), f32), dma((columns // wide + 2,))],
+        jnp.transpose(cloud_state, (1, 0, 2)),
+        model_to_cloud_levels,
+        cloud_to_model_levels.T,
+        hbm_in=range(3),
+        cost=pl.CostEstimate(flops=10**8, bytes_accessed=4 * 10**6, transcendentals=0),
     )
     by_column = exchange(arranged)
     cloud_next, fed = kernel_call(
-        functools.partial(cloud_kernel, depth=depth, levels=levels),
+        functools.partial(cloud_kernel, depth=depth, levels=levels, wide=wide),
         "cloud",
         (shape((clev, variables, width), f32), flat),
         [
             pltpu.VMEM((clev * variables, LANES), f32),
             pltpu.VMEM((clev * variables, LANES), f32),
+            pltpu.VMEM((clev, variables, width), f32),
+            dma,
         ],
         by_column.reshape(flat.shape),
-        model_to_cloud_levels,
-        cloud_to_model_levels,
-        jnp.transpose(cloud_state, (1, 0, 2)),
+        base,
+        mean,
+        down,
+        up,
+        hbm_out=(0,),
     )
     fed_level = exchange(fed.reshape(slots.shape))
-    advanced = kernel_call(
+    (advanced,) = kernel_call(
         functools.partial(update_kernel, share=share),
         "update",
-        slots,
+        (slots,),
         [pltpu.VMEM(pairs.shape, f32)],
         fed_level,
         partial,
     )
     home = exchange(advanced)
-    model_next = kernel_call(
+    (model_next,) = kernel_call(
         functools.partial(unpack_kernel, depth=depth),
         "unpack_state",
-        shape(model_state.shape, f32),
+        (shape(model_state.shape, f32),),
         [],
         home.reshape(flat.shape),
     )

time: 73.2 us -> 57.5 us (0.79)
  Pallas kernels: 21.4 us -> 13.5 us
  blocking collectives: 39.1 us -> 35.7 us
  waiting for transfers between devices: 6.93 us -> 4.81 us
  local copies, waits for them, and re-layouts: 2.1 us -> 0 us
    pallas_call x5 -> x6, Pallas kernels: 21.4 us -> 13.5 us  [kernel_call(): pl.pallas_call(body, name=name, out_shape=results, in_specs=[spec[n in hb...]
    all_to_all x3, blocking collectives: 39.1 us -> 35.7 us  [exchange(): return lax.all_to_all(slots, AXES, split_axis=0, concat_axis=0, tiled=True)]
    all_to_all x1, waiting for transfers between devices: 6.93 us -> 4.81 us  [exchange(): return lax.all_to_all(slots, AXES, split_axis=0, concat_axis=0, tiled=True)]
    unnamed x3 -> x0, local copies, waits for them, and re-layouts: 2.1 us -> none
  transfers between devices with their start and end apart: 1 -> 1, of which waited for: 1 -> 1; matrix products, arithmetic and copies ran while one was open for 2% -> 0% of each run, Pallas kernels for 0% -> 6%
where the time goes in v2:
time: 57.5 us; the launch traced here: 57.2 us
  blocking collectives  35.7 us (62%)
  Pallas kernels  13.5 us (23%)
  waiting for transfers between devices  4.81 us (8%)
  starting transfers between devices  2.58 us (4%)
  between operations  0.67 us (1%)
    all_to_all x3, blocking collectives, exchange(): return lax.all_to_all(slots, AXES, split_axis=0, concat_axis=0, tiled=True)  35.7 us
    pallas_call x6, Pallas kernels, kernel_call(): pl.pallas_call(body, name=name, out_shape=results, in_specs=[spec[n in hb...  13.5 us
    all_to_all x1, waiting for transfers between devices, exchange(): return lax.all_to_all(slots, AXES, split_axis=0, concat_axis=0, tiled=True)  4.81 us
    all_to_all x1, starting transfers between devices, exchange(): return lax.all_to_all(slots, AXES, split_axis=0, concat_axis=0, tiled=True)  2.58 us
  transfers between devices with their start and end apart: 1, of which 1 were waited for; matrix products, arithmetic and copies ran while one was open for 0% of the time, Pallas kernels for 6%

profile of v2, /device:TPU:0, one launch (start us, length us, event | category | flops | bytes accessed | tf_op | source)
XLA Modules:
  0.0 57.2 jit_solution(1368823822148640583)
XLA Ops:
  0.6 1.1 %pack_state.1 = (f32[256,128]{1,0:T(8,128)S(1)}, f32[128,256]{1,0:T(8,128)S(1)}) custom-call(s32[4,4]{1,0:T(4,128)} %nbr_hbm.1, s32[4,4]{1,0:T(4,128)} %face_hbm.1, s32[1,256]{1,0:T(1,128)} %order_hbm.1, f32[4,4,16,72]{3,2,1,0:T(8,128)} %state_hbm.1, f32[128,256]{1,0:T(8,128)} %constant.2.clone.weight_hbm), custom_call_target="tpu_custom_call" | custom-call | tf_op jit(solution)/shard_map/pack_state/pallas_call | solution.py:549
  1.8 15.5 %all_to_all.20.got_ref = f32[32,8,128]{2,1,0:T(8,128)S(1)} all-to-all(f32[32,8,128]{2,1,0:T(8,128)S(1)} %bitcast.10), channel_id=1, replica_groups=mesh['cols'=8,'vars'=4] {'cols','vars'}, dimensions={0} | all-to-all | bytes 262144 | tf_op jit(solution)/shard_map/all_to_all | solution.py:562
  17.3 1.8 %tendency.1 = (f32[32,8,128]{2,1,0:T(8,128)}, f32[16,2,8,128]{3,2,1,0:T(8,128)S(1)}) custom-call(f32[32,8,128]{2,1,0:T(8,128)S(1)} %all_to_all.20.got_ref, f32[128,256]{1,0:T(8,128)S(1)} %get-tuple-element.13.weight_ref), custom_call_target="tpu_custom_call" | custom-call | tf_op jit(solution)/shard_map/tendency/pallas_call | solution.py:549
  19.1 2.6 %all-to-all-start.1 = ((f32[32,8,128]{2,1,0:T(8,128)}), f32[32,8,128]{2,1,0:T(8,128)S(1)}, u32[]{:S(2)}, u32[]{:S(2)}) async-start(f32[32,8,128]{2,1,0:T(8,128)} %get-tuple-element.14), calls=%async_computation.1 | async-start | bytes 262144 | tf_op jit(solution)/shard_map/all_to_all | solution.py:562
  21.7 3.6 %settle.1 = (f32[200,2048]{1,0:T(8,128)S(1)}, f32[200,128]{1,0:T(8,128)S(1)}, f32[50,72]{1,0:T(8,128)S(1)}, f32[50,72]{1,0:T(8,128)S(1)}) custom-call(f32[50,4,2048]{2,1,0:T(4,128)} %bitcast.11, f32[50,72]{1,0:T(8,128)} %down_hbm.1, f32[50,72]{1,0:T(8,128)} %bitcast.12), custom_call_target="tpu_custom_call" | custom-call | flops 100000000 | bytes 4000000 | tf_op jit(solution)/shard_map/settle/pallas_call | solution.py:549
  25.3 4.8 %all-to-all-done.1 = f32[32,8,128]{2,1,0:T(8,128)S(1)} async-done(((f32[32,8,128]{2,1,0:T(8,128)}), f32[32,8,128]{2,1,0:T(8,128)S(1)}, u32[]{:S(2)}, u32[]{:S(2)}) %all-to-all-start.1) | async-done | bytes 131104 | tf_op jit(solution)/shard_map/all_to_all | solution.py:562
  30.1 4.1 %cloud.1 = (f32[50,4,2048]{2,1,0:T(4,128)}, f32[256,128]{1,0:T(8,128)S(1)}) custom-call(f32[256,128]{1,0:T(8,128)S(1)} %bitcast.8, f32[200,2048]{1,0:T(8,128)S(1)} %get-tuple-element.15.base_ref, f32[200,128]{1,0:T(8,128)S(1)} %get-tuple-element.16.mean_ref, f32[50,72]{1,0:T(8,128)S(1)} %get-tuple-element.17.down_ref, f32[50,72]{1,0:T(8,128)S(1)} %get-tuple-element.18.up_ref), custom_call_target="tpu_custom_call" | custom-call | tf_op jit(solution)/shard_map/cloud/pallas_call | solution.py:549
  34.1 10.1 %all_to_all.21.got_ref = f32[32,8,128]{2,1,0:T(8,128)S(1)} all-to-all(f32[32,8,128]{2,1,0:T(8,128)S(1)} %bitcast.9), channel_id=1, replica_groups=mesh['cols'=8,'vars'=4] {'cols','vars'}, dimensions={0} | all-to-all | bytes 262144 | tf_op jit(solution)/shard_map/all_to_all | solution.py:562
  44.2 2.2 %update.1 = f32[32,8,128]{2,1,0:T(8,128)S(1)} custom-call(f32[32,8,128]{2,1,0:T(8,128)S(1)} %all_to_all.21.got_ref, f32[16,2,8,128]{3,2,1,0:T(8,128)S(1)} %get-tuple-element.20.partial_ref), custom_call_target="tpu_custom_call" | custom-call | tf_op jit(solution)/shard_map/update/pallas_call | solution.py:549
  46.4 10.1 %all_to_all.22 = f32[32,8,128]{2,1,0:T(8,128)S(1)} all-to-all(f32[32,8,128]{2,1,0:T(8,128)S(1)} %update.1), channel_id=1, replica_groups=mesh['cols'=8,'vars'=4] {'cols','vars'}, dimensions={0} | all-to-all | bytes 262144 | tf_op jit(solution)/shard_map/all_to_all | solution.py:562
  56.5 0.8 %unpack_state.1 = f32[4,4,16,72]{3,2,1,0:T(8,128)} custom-call(f32[256,128]{1,0:T(8,128)S(1)} %bitcast.7), custom_call_target="tpu_custom_call" | custom-call | tf_op jit(solution)/shard_map/unpack_state/pallas_call | solution.py:549
Async XLA Ops:
  19.1 11.0 %all-to-all-start.1 = ((f32[32,8,128]{2,1,0:T(8,128)}), f32[32,8,128]{2,1,0:T(8,128)S(1)}, u32[]{:S(2)}, u32[]{:S(2)}) async-start(f32[32,8,128]{2,1,0:T(8,128)} %get-tuple-element.14), calls=%async_computation.1 | async-start | bytes 262144 | tf_op jit(solution)/shard_map/all_to_all | solution.py:562

commit v3 on v2

v3 whole, which is shorter than its diff:
```python
import functools

import jax
import jax.numpy as jnp
import numpy as np
from jax import lax
from jax.experimental import pallas as pl
from jax.experimental.pallas import tpu as pltpu
from jax.sharding import PartitionSpec as P

CCOL = 32
NODES = 16
LANES = 128
ROWS = 8
AXES = ("cols", "vars")
VISCOSITY = 0.01
DRIFT = 0.05
PENALTY = 0.5
TIME_STEP = 0.5
CLOUD_ADVECT = 0.25
CLOUD_DIFFUSE = 0.1
CONDENSE_RATE = 0.3
SATURATION_BASE = 0.5
SATURATION_SLOPE = 0.3
RETAIN = 0.8
EXACT = lax.Precision.HIGHEST
KERNEL_VMEM = 16 * 2**20
WIDE = 2
GROUP = 16
SWAPS = 4
FAR_ROW = 6
ORDER_ROW = 7


def lobatto_derivative():
    points = np.array([-1.0, -1.0 / np.sqrt(5.0), 1.0 / np.sqrt(5.0), 1.0])
    derivative = np.zeros((4, 4))
    for target in range(4):
        for source in range(4):
            if target != source:
                weight_target = np.prod(
                    [points[target] - points[middle] for middle in range(4) if middle != target]
                )
                weight_source = np.prod(
                    [points[source] - points[middle] for middle in range(4) if middle != source]
                )
                derivative[target, source] = weight_target / (
                    weight_source * (points[target] - points[source])
                )
        derivative[target, target] = np.sum(
            [1.0 / (points[target] - points[middle]) for middle in range(4) if middle != target]
        )
    return derivative


def node_weights():
    derivative = lobatto_derivative()
    along_first = np.kron(np.eye(4), derivative)
    along_second = np.kron(derivative, np.eye(4))
    laplace = along_first @ along_first + along_second @ along_second
    edges = np.zeros((4, 4))
    edges[0, :] += 1.0
    edges[3, :] += 1.0
    edges[:, 0] += 1.0
    edges[:, 3] += 1.0
    linear = VISCOSITY * laplace - PENALTY * np.diag(edges.reshape(-1))
    repeat = np.eye(LANES // NODES)
    weights = np.concatenate(
        [np.kron(repeat, linear.T), np.kron(repeat, -DRIFT * along_first.T)], axis=1
    )
    high = weights.astype(jnp.bfloat16)
    low = (weights - high.astype(np.float64)).astype(jnp.bfloat16)
    return jnp.asarray(np.stack([high, low]))


def each(count, body, group=GROUP):
    group = min(group, count)
    if count <= group:
        for index in range(count):
            body(index)
        return

    def several(first, carry):
        for n in range(group):
            body(first * group + n)
        return carry

    lax.fori_loop(0, count // group, several, 0)


def lane_ids(rows=ROWS):
    return lax.broadcasted_iota(jnp.int32, (rows, LANES), 1)


def row_ids():
    return lax.broadcasted_iota(jnp.int32, (ROWS, LANES), 0)


def pick(values, lanes):
    return jnp.take_along_axis(values, lanes, axis=1, mode="promise_in_bounds")


def half_turn(values):
    return pltpu.roll(values, LANES // 2, 1)


def split_pair(first, second):
    lower = lane_ids() < LANES // 2
    return (
        jnp.where(lower, first, half_turn(second)),
        jnp.where(lower, half_turn(first), second),
    )


def row_of(values, row):
    return jnp.broadcast_to(values[row : row + 1], (ROWS, LANES))


def unpack_pairs(got_ref, field):
    def unpack(q):
        low, high = split_pair(got_ref[2 * q], got_ref[2 * q + 1])
        field[q, 0] = low
        field[q, 1] = high

    each(field.shape[0], unpack)


def pack_pair(out_ref, q, low, high):
    first, second = split_pair(low, high)
    out_ref[2 * q] = first
    out_ref[2 * q + 1] = second


def swap_groups(source, target, share):
    groups = LANES // share
    group = lane_ids() // share

    def swap(index):
        x = index // 2
        y = index % 2

        def gather(w):
            for part in range(2):
                joined = source[2 * groups * x + y, part]
                joined = pltpu.roll(joined, (LANES - share * w) % LANES, 1)
                for u in range(1, groups):
                    other = source[2 * (groups * x + u) + y, part]
                    turned = pltpu.roll(other, (share * (u + groups - w)) % LANES, 1)
                    joined = jnp.where(group == u, turned, joined)
                target[2 * (groups * y + w) + x, part] = joined

        each(groups, gather)

    each(4, swap, SWAPS)


def reorder(source, block_tile, places):
    spot = places & (LANES - 1)
    first = places < LANES
    return [
        jnp.where(
            first,
            pick(source[block_tile, part], spot),
            pick(source[block_tile + 1, part], spot),
        )
        for part in range(2)
    ]


def pack_kernel(
    nbr_hbm,
    face_hbm,
    order_hbm,
    state_hbm,
    weight_hbm,
    out_ref,
    weight_ref,
    nbr_ref,
    face_ref,
    order_ref,
    state_ref,
    scratch,
    sems,
    depth,
    block,
):
    copies = [
        pltpu.make_async_copy(source, target, sems.at[n])
        for n, (source, target) in enumerate(
            (
                (nbr_hbm, nbr_ref),
                (face_hbm, face_ref),
                (order_hbm, order_ref),
                (state_hbm, state_ref),
                (weight_hbm, weight_ref),
            )
        )
    ]
    for copy in copies:
        copy.start()
    elements, variables, nodes, levels = state_ref.shape
    used = levels // depth
    half = LANES // 2
    lane = lane_ids()
    own = lax.axis_index("vars")
    column = lane % half
    elem = column // nodes
    along_y = (column // 4) % 4
    along_x = column % 4
    upper = lane >= half
    edge = jnp.where(
        upper,
        jnp.where(along_x == 3, 1, jnp.where(along_x == 0, 3, -1)),
        jnp.where(along_y == 0, 0, jnp.where(along_y == 3, 2, -1)),
    )
    along = jnp.where(upper, along_y, along_x)
    place = jnp.where(edge >= 2, 3 - along, along)
    out_ref[...] = jnp.zeros_like(out_ref)
    copies[0].wait()
    copies[1].wait()
    far = jnp.zeros_like(lane)
    face = jnp.zeros_like(lane)
    for e in range(elements):
        for j in range(4):
            here = (elem == e) & (edge == j)
            far = jnp.where(here, nbr_ref[e, j], far)
            face = jnp.where(here, face_ref[e, j], face)
    node = jnp.where(
        face == 0,
        3 - place,
        jnp.where(face == 1, 15 - 4 * place, jnp.where(face == 2, 12 + place, 4 * place)),
    )
    far_col = jnp.where(edge >= 0, nodes * far + node, -1).astype(jnp.float32)

    copies[2].wait()
    order = order_ref[...]
    spots = lax.broadcasted_iota(jnp.int32, (block, block), 0)
    marks = (spots == order).astype(jnp.float32).astype(jnp.bfloat16)
    numbers = lax.broadcasted_iota(jnp.int32, (ROWS, block), 1).astype(jnp.float32)
    scratch[0] = jnp.broadcast_to(order, (ROWS, block)).astype(jnp.float32)
    scratch[1] = lax.dot_general(
        numbers.astype(jnp.bfloat16),
        marks,
        (((1,), (1,)), ((), ())),
        preferred_element_type=jnp.float32,
    )
    begin = pl.multiple_of((own // 2) * LANES, LANES)
    order_part = scratch[0, :, pl.ds(begin, LANES)]
    place_part = scratch[1, :, pl.ds(begin, LANES)]
    odd = own % 2 == 1
    order_part = jnp.where(odd, half_turn(order_part), order_part)
    place_part = jnp.where(odd, place_part, half_turn(place_part))
    indices = jnp.where(upper, place_part, order_part)

    slots = out_ref.shape[0] // ROWS
    for first in range(0, slots, ROWS):
        out_ref[pl.ds(ROWS * first + FAR_ROW, ROWS, stride=ROWS), :] = far_col
        out_ref[pl.ds(ROWS * first + ORDER_ROW, ROWS, stride=ROWS), :] = indices
    copies[3].wait()
    for pair in range(variables // 2):
        fields = jnp.concatenate(
            [
                state_ref[:, pair].reshape(elements * nodes, levels),
                state_ref[:, variables // 2 + pair].reshape(elements * nodes, levels),
            ],
            axis=0,
        )
        by_level = fields.T
        for part in range(depth):
            for first in range(0, used, ROWS):
                begin = used * part + first
                out_ref[pl.ds(ROWS * first + depth * pair + part, ROWS, stride=ROWS), :] = (
                    by_level[begin : begin + ROWS]
                )
    copies[4].wait()


def tendency_kernel(
    got_ref, weight_ref, out_ref, partial_ref, field, linear, tend, moved, depth, share
):
    tiles = field.shape[0]
    row = row_ids()
    lower = lane_ids() < LANES // 2
    unpack_pairs(got_ref, field)
    step = min(tiles, 16)

    def multiply(chunk):
        fields = field[pl.ds(chunk * step, step)].reshape(step * 2 * ROWS, LANES)
        high, low = in_two(fields)
        coarse, fine = weight_ref[0], weight_ref[1]
        result = jnp.dot(
            jnp.concatenate([high, low], axis=1),
            jnp.concatenate([coarse, coarse], axis=0),
            preferred_element_type=jnp.float32,
        ) + jnp.dot(high, fine, preferred_element_type=jnp.float32)
        linear[pl.ds(chunk * step, step)] = result.reshape(step, 2, ROWS, 2 * LANES)

    each(tiles // step, multiply, 1)

    def advance(q):
        before = jnp.where(q == 0, tiles - 1, q - 1)
        after = jnp.where(q == tiles - 1, 0, q + 1)
        high = field[q, 1]
        wind = jnp.where(row < depth, pltpu.roll(high, ROWS - depth, 0), high)
        sums = [0.0, 0.0]
        for side in range(2):
            far = row_of(field[q, side], FAR_ROW).astype(jnp.int32)
            spot = far & (LANES - 1)
            inside = lax.shift_right_arithmetic(far, 7) == q
            for part in range(2):
                beside = jnp.where(lower, field[after, part], field[before, part])
                value = jnp.where(inside, pick(field[q, part], spot), pick(beside, spot))
                sums[part] = sums[part] + jnp.where(far >= 0, value, 0.0)
        for part in range(2):
            own = field[q, part]
            result = (
                linear[q, part, :, :LANES]
                + wind * linear[q, part, :, LANES:]
                + PENALTY * sums[part]
            )
            tend[q, part] = result
            partial_ref[q, part] = jnp.where(row < FAR_ROW, own + TIME_STEP * result, own)

    each(tiles, advance)
    swap_groups(tend, moved, share)

    def arrange(p):
        order = row_of(field[p, 0], ORDER_ROW).astype(jnp.int32)
        pack_pair(out_ref, p, *reorder(moved, p // 2 * 2, order))

    each(tiles, arrange)


def in_two(values):
    high = values.astype(jnp.bfloat16)
    low = (values - high.astype(jnp.float32)).astype(jnp.bfloat16)
    return high, low


def pool_weights(step):
    wide = WIDE * LANES
    lane = lax.broadcasted_iota(jnp.int32, (wide, LANES), 1) % (LANES // 2)
    owner = lax.broadcasted_iota(jnp.int32, (wide, LANES), 0) // CCOL
    mean = 1.0 / (CCOL * TIME_STEP)
    return jnp.where(lane == (wide // CCOL) * step + owner, mean, 0.0).astype(jnp.bfloat16)


def pooled_sum(tiles, weights):
    joined = jnp.concatenate([jnp.concatenate(tile, axis=0) for tile in tiles], axis=1)
    rows = joined.shape[0]
    both = jnp.concatenate(in_two(joined), axis=0)
    result = jnp.dot(both, weights, preferred_element_type=jnp.float32)
    return result[:rows] + result[rows:]


def settle_kernel(
    cloud_hbm,
    down_hbm,
    up_hbm,
    base_ref,
    mean_ref,
    pool_ref,
    down_ref,
    up_ref,
    cloud_ref,
    sums,
    sems,
):
    columns, variables, deep = base_ref.shape[:3]
    clev = cloud_hbm.shape[0]
    plane = (columns + 1) * variables
    steps = columns // WIDE
    small = [
        pltpu.make_async_copy(down_hbm, down_ref, sems.at[steps]),
        pltpu.make_async_copy(up_hbm, up_ref, sems.at[steps + 1]),
    ]

    def fetch(step):
        here = pl.ds(WIDE * step, WIDE)
        return pltpu.make_async_copy(
            cloud_hbm.at[:, here], cloud_ref.at[pl.ds(1, clev), here], sems.at[step]
        )

    for step in range(steps):
        fetch(step).start()
    for copy in small:
        copy.start()
    flat_ref = cloud_ref.reshape((deep + 2) * plane, LANES)
    rim = jnp.zeros((plane, LANES), jnp.float32)
    flat_ref[0:plane] = rim
    for level in range(clev, deep + 1):
        flat_ref[(level + 1) * plane : (level + 2) * plane] = rim
    sums[...] = jnp.zeros_like(sums)
    within = lane_ids() % CCOL
    last = within == CCOL - 1
    first = within == 0

    def tile(t):
        def load(level, variable):
            begin = (level + 1) * plane + variables * t + variable
            return flat_ref[pl.ds(begin, ROWS, stride=plane), :]

        changes = []
        winds = [
            (-CLOUD_ADVECT * TIME_STEP) * load(level, 3) for level in range(0, deep, ROWS)
        ]
        for variable in range(variables):
            for level in range(0, deep, ROWS):
                now = load(level, variable)
                ahead = jnp.where(
                    last, pltpu.roll(now, CCOL - 1, 1), pltpu.roll(now, LANES - 1, 1)
                )
                behind = jnp.where(
                    first, pltpu.roll(now, LANES - CCOL + 1, 1), pltpu.roll(now, 1, 1)
                )
                around = load(level - 1, variable) + load(level + 1, variable)
                change = winds[level // ROWS] * (ahead - behind) + (
                    CLOUD_DIFFUSE * TIME_STEP
                ) * (around - 2.0 * now)
                base = now + change
                base_ref[t, variable, level : level + ROWS, :] = base
                changes.append(RETAIN * base - now if variable == 2 else change)
        return changes

    def advance(step, carry):
        fetch(step).wait()
        weights = pool_weights(step)
        pool_ref[step] = weights
        sums[...] += pooled_sum([tile(WIDE * step + n) for n in range(WIDE)], weights)
        return carry

    lax.fori_loop(0, steps, advance, 0)
    lower = lane_ids(deep) < LANES // 2
    for pair in range(2):
        mean_ref[pair] = jnp.where(
            lower,
            sums[deep * pair : deep * (pair + 1)],
            sums[deep * (2 + pair) : deep * (3 + pair)],
        )
    for copy in small:
        copy.wait()


def cloud_kernel(
    got_ref,
    base_ref,
    mean_ref,
    pool_ref,
    down_ref,
    up_ref,
    next_hbm,
    out_ref,
    forced,
    sums,
    next_ref,
    sem,
    depth,
):
    columns, variables, deep = base_ref.shape[:3]
    clev, levels = down_ref.shape
    plane = (columns + 1) * variables
    flat_ref = next_ref.reshape(clev * plane, LANES)
    steps = columns // WIDE
    used = levels // depth
    half = LANES // 2
    fields = jnp.concatenate(
        [
            jnp.concatenate(
                [
                    got_ref[pl.ds(ROWS * first + depth * pair + part, ROWS, stride=ROWS), :]
                    for part in range(depth)
                    for first in range(0, used, ROWS)
                ],
                axis=0,
            )
            for pair in range(2)
        ],
        axis=1,
    )
    forcing = jnp.dot(TIME_STEP * down_ref[...], fields, precision=EXACT)
    for pair in range(2):
        forced[pair, 0:clev] = forcing[:, LANES * pair : LANES * pair + LANES]
        forced[pair, clev:deep] = jnp.zeros((deep - clev, LANES), jnp.float32)
    sums[...] = jnp.zeros_like(sums)
    owner = lane_ids() // CCOL

    def tile(t):
        near = (LANES // CCOL) * t + owner
        spots = (near, near, near + half, near + half)
        results = []
        for level in range(0, deep, ROWS):
            source = [forced[pair, level : level + ROWS, :] for pair in range(2)]
            moved = [
                base_ref[t, variable, level : level + ROWS, :]
                + pick(source[variable % 2], spots[variable])
                for variable in range(variables)
            ]
            excess = moved[1] - SATURATION_BASE * jnp.exp(SATURATION_SLOPE * moved[0])
            soft = jnp.maximum(excess, 0.0) + jnp.log(1.0 + jnp.exp(-jnp.abs(excess)))
            condensed = CONDENSE_RATE * soft
            updated = (
                moved[0] + condensed,
                moved[1] - condensed,
                RETAIN * moved[2] + condensed,
                moved[3],
            )
            count = min(ROWS, clev - level)
            for variable in range(variables):
                begin = level * plane + variables * t + variable
                flat_ref[pl.ds(begin, count, stride=plane), :] = updated[variable][:count]
            results.append(condensed)
        return results

    def store(begin, count):
        here = pl.ds(begin, count)
        return pltpu.make_async_copy(next_ref.at[:, here], next_hbm.at[:, here], sem)

    def advance(step, carry):
        results = [tile(WIDE * step + n) for n in range(WIDE)]
        store(WIDE * step, WIDE).start()
        sums[...] += pooled_sum(results, pool_ref[step])
        return carry

    lax.fori_loop(0, steps, advance, 0)
    lower = lane_ids(clev) < half
    extra = sums[0:clev]
    share = 1.0 / TIME_STEP
    first = mean_ref[0, 0:clev] + jnp.where(lower, share, share * RETAIN) * forced[0, 0:clev]
    first = first + extra
    second = mean_ref[1, 0:clev] + share * forced[1, 0:clev] - jnp.where(lower, extra, 0.0)
    feedback = lax.dot_general(
        up_ref[...],
        jnp.concatenate([first, second], axis=1),
        (((0,), (0,)), ((), ())),
        precision=EXACT,
    )
    for pair in range(2):
        for part in range(depth):
            for first in range(0, used, ROWS):
                begin = used * part + first
                out_ref[pl.ds(ROWS * first + depth * pair + part, ROWS, stride=ROWS), :] = (
                    feedback[begin : begin + ROWS, LANES * pair : LANES * pair + LANES]
                )
    store(0, columns).wait()


def update_kernel(got_ref, partial_ref, out_ref, field, sorted_ref, share):
    tiles = field.shape[0]
    unpack_pairs(got_ref, field)

    def collect(p):
        place = row_of(partial_ref[p, 1], ORDER_ROW).astype(jnp.int32)
        for part, values in enumerate(reorder(field, p // 2 * 2, place)):
            sorted_ref[p, part] = values

    each(tiles, collect)
    swap_groups(sorted_ref, field, share)

    def finish(q):
        pack_pair(
            out_ref,
            q,
            partial_ref[q, 0] + TIME_STEP * field[q, 0],
            partial_ref[q, 1] + TIME_STEP * field[q, 1],
        )

    each(tiles, finish)


def unpack_kernel(got_ref, state_ref, depth):
    elements, variables, nodes, levels = state_ref.shape
    used = levels // depth
    for pair in range(variables // 2):
        by_level = jnp.concatenate(
            [
                got_ref[pl.ds(ROWS * first + depth * pair + part, ROWS, stride=ROWS), :]
                for part in range(depth)
                for first in range(0, used, ROWS)
            ],
            axis=0,
        )
        fields = by_level.T.reshape(2, elements, nodes, levels)
        state_ref[:, pair] = fields[0]
        state_ref[:, variables // 2 + pair] = fields[1]


def kernel_call(body, name, results, scratch, *operands, hbm_in=(), hbm_out=(), cost=None):
    spec = {True: pl.BlockSpec(memory_space=pltpu.HBM), False: pl.BlockSpec(memory_space=pltpu.VMEM)}
    operands = [
        pltpu.with_memory_space_constraint(value, pltpu.HBM) if n in hbm_in else value
        for n, value in enumerate(operands)
    ]
    return pl.pallas_call(
        body,
        name=name,
        out_shape=results,
        in_specs=[spec[n in hbm_in] for n in range(len(operands))],
        out_specs=tuple(spec[n in hbm_out] for n in range(len(results))),
        scratch_shapes=scratch,
        cost_estimate=cost,
        compiler_params=pltpu.CompilerParams(vmem_limit_bytes=KERNEL_VMEM),
    )(*operands)


def exchange(slots):
    return lax.all_to_all(slots, AXES, split_axis=0, concat_axis=0, tiled=True)


def shards(
    model_state,
    cloud_state,
    neighbor,
    facing_edge,
    column_order,
    model_to_cloud_levels,
    cloud_to_model_levels,
):
    elements, variables, nodes, levels = model_state.shape
    clev, width = cloud_state.shape[1:]
    devices = lax.axis_size(AXES)
    block = column_order.shape[1]
    share = block // lax.axis_size("cols")
    depth = -(-levels // devices)
    assert variables == 4 and nodes == NODES and 2 * elements * nodes == LANES
    assert 2 * depth <= FAR_ROW and levels % (ROWS * depth) == 0 and block == 2 * LANES
    tiles = devices // 2
    f32 = jnp.float32
    shape = jax.ShapeDtypeStruct
    flat = shape((devices * ROWS, LANES), f32)
    slots = shape((devices, ROWS, LANES), f32)
    pairs = shape((tiles, 2, ROWS, LANES), f32)
    columns = width // LANES
    assert columns % WIDE == 0 and columns % 2 == 0
    deep = -(-clev // ROWS) * ROWS
    dma = pltpu.SemaphoreType.DMA

    packed, weights = kernel_call(
        functools.partial(pack_kernel, depth=depth, block=block),
        "pack_state",
        (flat, shape((2, LANES, 2 * LANES), jnp.bfloat16)),
        [
            pltpu.SMEM(neighbor.shape, jnp.int32),
            pltpu.SMEM(facing_edge.shape, jnp.int32),
            pltpu.VMEM(column_order.shape, jnp.int32),
            pltpu.VMEM(model_state.shape, f32),
            pltpu.VMEM((2, ROWS, block), f32),
            dma((5,)),
        ],
        neighbor,
        facing_edge,
        column_order,
        model_state,
        node_weights(),
        hbm_in=range(5),
    )
    by_level = exchange(packed.reshape(slots.shape))
    arranged, partial = kernel_call(
        functools.partial(tendency_kernel, depth=depth, share=share),
        "tendency",
        (slots, pairs),
        [
            pltpu.VMEM(pairs.shape, f32),
            pltpu.VMEM((tiles, 2, ROWS, 2 * LANES), f32),
            pltpu.VMEM(pairs.shape, f32),
            pltpu.VMEM(pairs.shape, f32),
        ],
        by_level,
        weights,
    )
    by_tile = cloud_state.reshape(variables, clev, columns, LANES).transpose(1, 2, 0, 3)
    base, mean, pool, down, up = kernel_call(
        settle_kernel,
        "settle",
        (
            shape((columns, variables, deep, LANES), f32),
            shape((2, deep, LANES), f32),
            shape((columns // WIDE, WIDE * LANES, LANES), jnp.bfloat16),
            shape((clev, levels), f32),
            shape((clev, levels), f32),
        ),
        [
            pltpu.VMEM((deep + 2, columns + 1, variables, LANES), f32),
            pltpu.VMEM((variables * deep, LANES), f32),
            dma((columns // WIDE + 2,)),
        ],
        by_tile,
        model_to_cloud_levels,
        cloud_to_model_levels.T,
        hbm_in=range(3),
        cost=pl.CostEstimate(flops=10**8, bytes_accessed=4 * 10**6, transcendentals=0),
    )
    by_column = exchange(arranged)
    cloud_next, fed = kernel_call(
        functools.partial(cloud_kernel, depth=depth),
        "cloud",
        (shape(by_tile.shape, f32), flat),
        [
            pltpu.VMEM((2, deep, LANES), f32),
            pltpu.VMEM((deep, LANES), f32),
            pltpu.VMEM((clev, columns + 1, variables, LANES), f32),
            dma,
        ],
        by_column.reshape(flat.shape),
        base,
        mean,
        pool,
        down,
        up,
        hbm_out=(0,),
    )
    fed_level = exchange(fed.reshape(slots.shape))
    (advanced,) = kernel_call(
        functools.partial(update_kernel, share=share),
        "update",
        (slots,),
        [pltpu.VMEM(pairs.shape, f32), pltpu.VMEM(pairs.shape, f32)],
        fed_level,
        partial,
    )
    home = exchange(advanced)
    (model_next,) = kernel_call(
        functools.partial(unpack_kernel, depth=depth),
        "unpack_state",
        (shape(model_state.shape, f32),),
        [],
        home.reshape(flat.shape),
    )
    cloud_next = cloud_next.transpose(2, 0, 1, 3).reshape(cloud_state.shape)
    return (model_next, cloud_next)


def solution(mesh):
    placed = (
        P(AXES, None, None, None),
        P(None, None, AXES),
        P(AXES, None),
        P(AXES, None),
        P("cols", None),
        P(),
        P(),
    )
    return jax.shard_map(
        shards,
        mesh=mesh,
        in_specs=placed,
        out_specs=(P(AXES, None, None, None), P(None, None, AXES)),
        check_vma=False,
    )
```

time: 57.5 us -> 54.4 us (0.946)
  Pallas kernels: 13.5 us -> 11.2 us
  waiting for transfers between devices: 4.81 us -> 3.85 us
    pallas_call x6, Pallas kernels: 13.5 us -> 11.2 us  [kernel_call(): pl.pallas_call(body, name=name, out_shape=results, in_specs=[spec[n in hb...]
    all_to_all x1, waiting for transfers between devices: 4.81 us -> 3.85 us  [exchange(): return lax.all_to_all(slots, AXES, split_axis=0, concat_axis=0, tiled=True)]
  transfers between devices with their start and end apart: 1 -> 1, of which waited for: 1 -> 1; matrix products, arithmetic and copies ran while one was open for 0% -> 0% of each run, Pallas kernels for 6% -> 8%
where the time goes in v3:
time: 54.4 us; the launch traced here: 54.1 us
  blocking collectives  35.8 us (66%)
  Pallas kernels  11.2 us (21%)
  waiting for transfers between devices  3.85 us (7%)
  starting transfers between devices  2.58 us (5%)
  between operations  0.67 us (1%)
    all_to_all x3, blocking collectives, exchange(): return lax.all_to_all(slots, AXES, split_axis=0, concat_axis=0, tiled=True)  35.8 us
    pallas_call x6, Pallas kernels, kernel_call(): pl.pallas_call(body, name=name, out_shape=results, in_specs=[spec[n in hb...  11.2 us
    all_to_all x1, waiting for transfers between devices, exchange(): return lax.all_to_all(slots, AXES, split_axis=0, concat_axis=0, tiled=True)  3.85 us
    all_to_all x1, starting transfers between devices, exchange(): return lax.all_to_all(slots, AXES, split_axis=0, concat_axis=0, tiled=True)  2.58 us
  transfers between devices with their start and end apart: 1, of which 1 were waited for; matrix products, arithmetic and copies ran while one was open for 0% of the time, Pallas kernels for 8%

profile of v3, /device:TPU:0, one launch (start us, length us, event | category | flops | bytes accessed | tf_op | source)
XLA Modules:
  0.0 54.1 jit_solution(346717351370263791)
XLA Ops:
  0.6 1.1 %pack_state.1 = (f32[256,128]{1,0:T(8,128)S(1)}, bf16[2,128,256]{2,1,0:T(8,128)(2,1)S(1)}) custom-call(s32[4,4]{1,0:T(4,128)} %nbr_hbm.1, s32[4,4]{1,0:T(4,128)} %face_hbm.1, s32[1,256]{1,0:T(1,128)} %order_hbm.1, f32[4,4,16,72]{3,2,1,0:T(8,128)} %state_hbm.1, bf16[2,128,256]{2,1,0:T(8,128)(2,1)} %constant.2.clone.weight_hbm), custom_call_target="tpu_custom_call" | custom-call | tf_op jit(solution)/shard_map/pack_state/pallas_call | solution.py:593
  1.8 15.5 %all_to_all.20.got_ref = f32[32,8,128]{2,1,0:T(8,128)S(1)} all-to-all(f32[32,8,128]{2,1,0:T(8,128)S(1)} %bitcast.14), channel_id=1, replica_groups=mesh['cols'=8,'vars'=4] {'cols','vars'}, dimensions={0} | all-to-all | bytes 262144 | tf_op jit(solution)/shard_map/all_to_all | solution.py:606
  17.3 1.4 %tendency.1 = (f32[32,8,128]{2,1,0:T(8,128)}, f32[16,2,8,128]{3,2,1,0:T(8,128)S(1)}) custom-call(f32[32,8,128]{2,1,0:T(8,128)S(1)} %all_to_all.20.got_ref, bf16[2,128,256]{2,1,0:T(8,128)(2,1)S(1)} %get-tuple-element.14.weight_ref), custom_call_target="tpu_custom_call" | custom-call | tf_op jit(solution)/shard_map/tendency/pallas_call | solution.py:593
  18.7 2.6 %all-to-all-start.1 = ((f32[32,8,128]{2,1,0:T(8,128)}), f32[32,8,128]{2,1,0:T(8,128)S(1)}, u32[]{:S(2)}, u32[]{:S(2)}) async-start(f32[32,8,128]{2,1,0:T(8,128)} %get-tuple-element.15), calls=%async_computation.1 | async-start | bytes 262144 | tf_op jit(solution)/shard_map/all_to_all | solution.py:606
  21.3 4.5 %settle.1 = (f32[16,4,56,128]{3,2,1,0:T(8,128)S(1)}, f32[2,56,128]{2,1,0:T(8,128)S(1)}, bf16[8,256,128]{2,1,0:T(8,128)(2,1)S(1)}, f32[50,72]{1,0:T(8,128)S(1)}, f32[50,72]{1,0:T(8,128)S(1)}) custom-call(f32[50,16,4,128]{3,2,1,0:T(4,128)} %bitcast.15, f32[50,72]{1,0:T(8,128)} %down_hbm.1, f32[50,72]{1,0:T(8,128)} %bitcast.16), custom_call_target="tpu_custom_call" | custom-call | flops 100000000 | bytes 4000000 | tf_op jit(solution)/shard_map/settle/pallas_call | solution.py:593
  25.9 3.9 %all-to-all-done.1 = f32[32,8,128]{2,1,0:T(8,128)S(1)} async-done(((f32[32,8,128]{2,1,0:T(8,128)}), f32[32,8,128]{2,1,0:T(8,128)S(1)}, u32[]{:S(2)}, u32[]{:S(2)}) %all-to-all-start.1) | async-done | bytes 131104 | tf_op jit(solution)/shard_map/all_to_all | solution.py:606
  29.7 2.9 %cloud.1 = (f32[50,16,4,128]{3,2,1,0:T(4,128)}, f32[256,128]{1,0:T(8,128)S(1)}) custom-call(f32[256,128]{1,0:T(8,128)S(1)} %bitcast.11, f32[16,4,56,128]{3,2,1,0:T(8,128)S(1)} %get-tuple-element.16.base_ref, f32[2,56,128]{2,1,0:T(8,128)S(1)} %get-tuple-element.17.mean_ref, bf16[8,256,128]{2,1,0:T(8,128)(2,1)S(1)} %get-tuple-element.18.pool_ref, ...), custom_call_target="tpu_custom_call" | custom-call | tf_op jit(solution)/shard_map/cloud/pallas_call | solution.py:593
  32.6 10.2 %all_to_all.21.got_ref = f32[32,8,128]{2,1,0:T(8,128)S(1)} all-to-all(f32[32,8,128]{2,1,0:T(8,128)S(1)} %bitcast.13), channel_id=1, replica_groups=mesh['cols'=8,'vars'=4] {'cols','vars'}, dimensions={0} | all-to-all | bytes 262144 | tf_op jit(solution)/shard_map/all_to_all | solution.py:606
  42.8 0.4 update.1
  43.3 10.1 %all_to_all.22 = f32[32,8,128]{2,1,0:T(8,128)S(1)} all-to-all(f32[32,8,128]{2,1,0:T(8,128)S(1)} %update.1), channel_id=1, replica_groups=mesh['cols'=8,'vars'=4] {'cols','vars'}, dimensions={0} | all-to-all | bytes 262144 | tf_op jit(solution)/shard_map/all_to_all | solution.py:606
  53.4 0.8 %unpack_state.1 = f32[4,4,16,72]{3,2,1,0:T(8,128)} custom-call(f32[256,128]{1,0:T(8,128)S(1)} %bitcast.12), custom_call_target="tpu_custom_call" | custom-call | tf_op jit(solution)/shard_map/unpack_state/pallas_call | solution.py:593
Async XLA Ops:
  18.7 11.0 %all-to-all-start.1 = ((f32[32,8,128]{2,1,0:T(8,128)}), f32[32,8,128]{2,1,0:T(8,128)S(1)}, u32[]{:S(2)}, u32[]{:S(2)}) async-start(f32[32,8,128]{2,1,0:T(8,128)} %get-tuple-element.15), calls=%async_computation.1 | async-start | bytes 262144 | tf_op jit(solution)/shard_map/all_to_all | solution.py:606

commit v4 on v3

--- a/solution.py
+++ b/solution.py
@@ -23,9 +23,11 @@
 SATURATION_BASE = 0.5
 SATURATION_SLOPE = 0.3
 RETAIN = 0.8
+LOG2_E = 1.4426950408889634
 EXACT = lax.Precision.HIGHEST
 KERNEL_VMEM = 16 * 2**20
-WIDE = 2
+WIDE = 8
+PIECE = 2
 GROUP = 16
 SWAPS = 4
 FAR_ROW = 6
@@ -104,8 +106,12 @@
     return pltpu.roll(values, LANES // 2, 1)
 
 
+def slot_rows(slot, rows):
+    return pl.ds(slot * rows, rows)
+
+
 def split_pair(first, second):
-    lower = lane_ids() < LANES // 2
+    lower = lane_ids(first.shape[0]) < LANES // 2
     return (
         jnp.where(lower, first, half_turn(second)),
         jnp.where(lower, half_turn(first), second),
@@ -117,18 +123,22 @@
 
 
 def unpack_pairs(got_ref, field):
+    rows = got_ref.shape[0] // (2 * field.shape[0])
+
     def unpack(q):
-        low, high = split_pair(got_ref[2 * q], got_ref[2 * q + 1])
-        field[q, 0] = low
-        field[q, 1] = high
+        low, high = split_pair(
+            got_ref[slot_rows(2 * q, rows), :], got_ref[slot_rows(2 * q + 1, rows), :]
+        )
+        field[q, 0, :rows] = low
+        field[q, 1, :rows] = high
 
     each(field.shape[0], unpack)
 
 
-def pack_pair(out_ref, q, low, high):
+def pack_pair(out_ref, q, rows, low, high):
     first, second = split_pair(low, high)
-    out_ref[2 * q] = first
-    out_ref[2 * q + 1] = second
+    out_ref[slot_rows(2 * q, rows), :] = first[:rows]
+    out_ref[slot_rows(2 * q + 1, rows), :] = second[:rows]
 
 
 def swap_groups(source, target, share):
@@ -326,7 +336,7 @@
 
     def arrange(p):
         order = row_of(field[p, 0], ORDER_ROW).astype(jnp.int32)
-        pack_pair(out_ref, p, *reorder(moved, p // 2 * 2, order))
+        pack_pair(out_ref, p, 2 * depth, *reorder(moved, p // 2 * 2, order))
 
     each(tiles, arrange)
 
@@ -360,6 +370,7 @@
     base_ref,
     mean_ref,
     pool_ref,
+    spread_ref,
     down_ref,
     up_ref,
     cloud_ref,
@@ -371,17 +382,18 @@
     plane = (columns + 1) * variables
     steps = columns // WIDE
     small = [
-        pltpu.make_async_copy(down_hbm, down_ref, sems.at[steps]),
-        pltpu.make_async_copy(up_hbm, up_ref, sems.at[steps + 1]),
+        pltpu.make_async_copy(down_hbm, down_ref, sems.at[columns // PIECE]),
+        pltpu.make_async_copy(up_hbm, up_ref, sems.at[columns // PIECE + 1]),
     ]
 
     def fetch(step):
-        here = pl.ds(WIDE * step, WIDE)
+        here = pl.ds(PIECE * step, PIECE)
         return pltpu.make_async_copy(
             cloud_hbm.at[:, here], cloud_ref.at[pl.ds(1, clev), here], sems.at[step]
         )
 
-    for step in range(steps):
+    pieces = columns // PIECE
+    for step in range(pieces):
         fetch(step).start()
     for copy in small:
         copy.start()
@@ -391,9 +403,14 @@
     for level in range(clev, deep + 1):
         flat_ref[(level + 1) * plane : (level + 2) * plane] = rim
     sums[...] = jnp.zeros_like(sums)
-    within = lane_ids() % CCOL
-    last = within == CCOL - 1
-    first = within == 0
+    column = lax.broadcasted_iota(jnp.int32, spread_ref.shape, 0) % LANES
+    place = lax.broadcasted_iota(jnp.int32, spread_ref.shape, 1)
+    column_of = (LANES // 2) * (place // LANES) + place % LANES // CCOL
+    spread_ref[...] = jnp.where(column == column_of, 1.0, 0.0).astype(jnp.bfloat16)
+    lane = lane_ids()
+    start = lane // CCOL * CCOL
+    next_lane = start + (lane + 1) % CCOL
+    last_lane = start + (lane + CCOL - 1) % CCOL
 
     def tile(t):
         def load(level, variable):
@@ -407,12 +424,8 @@
         for variable in range(variables):
             for level in range(0, deep, ROWS):
                 now = load(level, variable)
-                ahead = jnp.where(
-                    last, pltpu.roll(now, CCOL - 1, 1), pltpu.roll(now, LANES - 1, 1)
-                )
-                behind = jnp.where(
-                    first, pltpu.roll(now, LANES - CCOL + 1, 1), pltpu.roll(now, 1, 1)
-                )
+                ahead = pick(now, next_lane)
+                behind = pick(now, last_lane)
                 around = load(level - 1, variable) + load(level + 1, variable)
                 change = winds[level // ROWS] * (ahead - behind) + (
                     CLOUD_DIFFUSE * TIME_STEP
@@ -423,10 +436,14 @@
         return changes
 
     def advance(step, carry):
-        fetch(step).wait()
         weights = pool_weights(step)
         pool_ref[step] = weights
-        sums[...] += pooled_sum([tile(WIDE * step + n) for n in range(WIDE)], weights)
+        results = []
+        for n in range(WIDE):
+            if n % PIECE == 0:
+                fetch((WIDE // PIECE) * step + n // PIECE).wait()
+            results.append(tile(WIDE * step + n))
+        sums[...] += pooled_sum(results, weights)
         return carry
 
     lax.fori_loop(0, steps, advance, 0)
@@ -446,6 +463,7 @@
     base_ref,
     mean_ref,
     pool_ref,
+    spread_ref,
     down_ref,
     up_ref,
     next_hbm,
@@ -462,12 +480,13 @@
     flat_ref = next_ref.reshape(clev * plane, LANES)
     steps = columns // WIDE
     used = levels // depth
+    rows = 2 * depth
     half = LANES // 2
     fields = jnp.concatenate(
         [
             jnp.concatenate(
                 [
-                    got_ref[pl.ds(ROWS * first + depth * pair + part, ROWS, stride=ROWS), :]
+                    got_ref[pl.ds(rows * first + depth * pair + part, ROWS, stride=rows), :]
                     for part in range(depth)
                     for first in range(0, used, ROWS)
                 ],
@@ -482,21 +501,28 @@
         forced[pair, 0:clev] = forcing[:, LANES * pair : LANES * pair + LANES]
         forced[pair, clev:deep] = jnp.zeros((deep - clev, LANES), jnp.float32)
     sums[...] = jnp.zeros_like(sums)
-    owner = lane_ids() // CCOL
+    high, low = in_two(jnp.concatenate([forced[0], forced[1]], axis=0))
 
     def tile(t):
-        near = (LANES // CCOL) * t + owner
-        spots = (near, near, near + half, near + half)
+        shift = LANES - (LANES // CCOL) * t
+        turned = [pltpu.roll(values, shift, 1) for values in (high, low)]
+        push = jnp.dot(
+            jnp.concatenate(turned, axis=1).astype(jnp.bfloat16),
+            spread_ref[...],
+            preferred_element_type=jnp.float32,
+        )
         results = []
         for level in range(0, deep, ROWS):
-            source = [forced[pair, level : level + ROWS, :] for pair in range(2)]
-            moved = [
-                base_ref[t, variable, level : level + ROWS, :]
-                + pick(source[variable % 2], spots[variable])
-                for variable in range(variables)
-            ]
-            excess = moved[1] - SATURATION_BASE * jnp.exp(SATURATION_SLOPE * moved[0])
-            soft = jnp.maximum(excess, 0.0) + jnp.log(1.0 + jnp.exp(-jnp.abs(excess)))
+            moved = []
+            for variable in range(variables):
+                begin = deep * (variable % 2) + level
+                lanes = LANES * (variable // 2)
+                moved.append(
+                    base_ref[t, variable, level : level + ROWS, :]
+                    + push[begin : begin + ROWS, lanes : lanes + LANES]
+                )
+            excess = moved[1] - SATURATION_BASE * jnp.exp2((SATURATION_SLOPE * LOG2_E) * moved[0])
+            soft = jnp.maximum(excess, 0.0) + jnp.log(1.0 + jnp.exp2(-LOG2_E * jnp.abs(excess)))
             condensed = CONDENSE_RATE * soft
             updated = (
                 moved[0] + condensed,
@@ -516,8 +542,11 @@
         return pltpu.make_async_copy(next_ref.at[:, here], next_hbm.at[:, here], sem)
 
     def advance(step, carry):
-        results = [tile(WIDE * step + n) for n in range(WIDE)]
-        store(WIDE * step, WIDE).start()
+        results = []
+        for n in range(WIDE):
+            results.append(tile(WIDE * step + n))
+            if (n + 1) % PIECE == 0:
+                store(WIDE * step + n + 1 - PIECE, PIECE).start()
         sums[...] += pooled_sum(results, pool_ref[step])
         return carry
 
@@ -538,7 +567,7 @@
         for part in range(depth):
             for first in range(0, used, ROWS):
                 begin = used * part + first
-                out_ref[pl.ds(ROWS * first + depth * pair + part, ROWS, stride=ROWS), :] = (
+                out_ref[pl.ds(rows * first + depth * pair + part, ROWS, stride=rows), :] = (
                     feedback[begin : begin + ROWS, LANES * pair : LANES * pair + LANES]
                 )
     store(0, columns).wait()
@@ -546,6 +575,7 @@
 
 def update_kernel(got_ref, partial_ref, out_ref, field, sorted_ref, share):
     tiles = field.shape[0]
+    rows = got_ref.shape[0] // (2 * tiles)
     unpack_pairs(got_ref, field)
 
     def collect(p):
@@ -560,6 +590,7 @@
         pack_pair(
             out_ref,
             q,
+            rows,
             partial_ref[q, 0] + TIME_STEP * field[q, 0],
             partial_ref[q, 1] + TIME_STEP * field[q, 1],
         )
@@ -573,7 +604,7 @@
     for pair in range(variables // 2):
         by_level = jnp.concatenate(
             [
-                got_ref[pl.ds(ROWS * first + depth * pair + part, ROWS, stride=ROWS), :]
+                got_ref[pl.ds(2 * depth * first + depth * pair + part, ROWS, stride=2 * depth), :]
                 for part in range(depth)
                 for first in range(0, used, ROWS)
             ],
@@ -602,8 +633,10 @@
     )(*operands)
 
 
-def exchange(slots):
-    return lax.all_to_all(slots, AXES, split_axis=0, concat_axis=0, tiled=True)
+def exchange(values, devices):
+    slots = values.reshape(devices, values.shape[0] // devices, 1, LANES)
+    moved = lax.all_to_all(slots, AXES, split_axis=0, concat_axis=0, tiled=True)
+    return moved.reshape(values.shape)
 
 
 def shards(
@@ -627,10 +660,10 @@
     f32 = jnp.float32
     shape = jax.ShapeDtypeStruct
     flat = shape((devices * ROWS, LANES), f32)
-    slots = shape((devices, ROWS, LANES), f32)
+    rows = shape((devices * 2 * depth, LANES), f32)
     pairs = shape((tiles, 2, ROWS, LANES), f32)
     columns = width // LANES
-    assert columns % WIDE == 0 and columns % 2 == 0
+    assert columns % WIDE == 0 and WIDE % PIECE == 0
     deep = -(-clev // ROWS) * ROWS
     dma = pltpu.SemaphoreType.DMA
 
@@ -653,11 +686,11 @@
         node_weights(),
         hbm_in=range(5),
     )
-    by_level = exchange(packed.reshape(slots.shape))
+    by_level = exchange(packed, devices)
     arranged, partial = kernel_call(
         functools.partial(tendency_kernel, depth=depth, share=share),
         "tendency",
-        (slots, pairs),
+        (rows, pairs),
         [
             pltpu.VMEM(pairs.shape, f32),
             pltpu.VMEM((tiles, 2, ROWS, 2 * LANES), f32),
@@ -668,20 +701,21 @@
         weights,
     )
     by_tile = cloud_state.reshape(variables, clev, columns, LANES).transpose(1, 2, 0, 3)
-    base, mean, pool, down, up = kernel_call(
+    base, mean, pool, spread, down, up = kernel_call(
         settle_kernel,
         "settle",
         (
             shape((columns, variables, deep, LANES), f32),
             shape((2, deep, LANES), f32),
             shape((columns // WIDE, WIDE * LANES, LANES), jnp.bfloat16),
+            shape((2 * LANES, 2 * LANES), jnp.bfloat16),
             shape((clev, levels), f32),
             shape((clev, levels), f32),
         ),
         [
             pltpu.VMEM((deep + 2, columns + 1, variables, LANES), f32),
             pltpu.VMEM((variables * deep, LANES), f32),
-            dma((columns // WIDE + 2,)),
+            dma((columns // PIECE + 2,)),
         ],
         by_tile,
         model_to_cloud_levels,
@@ -689,41 +723,42 @@
         hbm_in=range(3),
         cost=pl.CostEstimate(flops=10**8, bytes_accessed=4 * 10**6, transcendentals=0),
     )
-    by_column = exchange(arranged)
+    by_column = exchange(arranged, devices)
     cloud_next, fed = kernel_call(
         functools.partial(cloud_kernel, depth=depth),
         "cloud",
-        (shape(by_tile.shape, f32), flat),
+        (shape(by_tile.shape, f32), rows),
         [
             pltpu.VMEM((2, deep, LANES), f32),
             pltpu.VMEM((deep, LANES), f32),
             pltpu.VMEM((clev, columns + 1, variables, LANES), f32),
             dma,
         ],
-        by_column.reshape(flat.shape),
+        by_column,
         base,
         mean,
         pool,
+        spread,
         down,
         up,
         hbm_out=(0,),
     )
-    fed_level = exchange(fed.reshape(slots.shape))
+    fed_level = exchange(fed, devices)
     (advanced,) = kernel_call(
         functools.partial(update_kernel, share=share),
         "update",
-        (slots,),
+        (rows,),
         [pltpu.VMEM(pairs.shape, f32), pltpu.VMEM(pairs.shape, f32)],
         fed_level,
         partial,
     )
-    home = exchange(advanced)
+    home = exchange(advanced, devices)
     (model_next,) = kernel_call(
         functools.partial(unpack_kernel, depth=depth),
         "unpack_state",
         (shape(model_state.shape, f32),),
         [],
-        home.reshape(flat.shape),
+        home,
     )
     cloud_next = cloud_next.transpose(2, 0, 1, 3).reshape(cloud_state.shape)
     return (model_next, cloud_next)

time: 54.4 us -> 51.9 us (0.954)
  Pallas kernels: 11.2 us -> 8.93 us
  blocking collectives: 35.8 us -> 34.7 us
  waiting for transfers between devices: 3.85 us -> 4.72 us
    pallas_call x6, Pallas kernels: 11.2 us -> 8.93 us  [kernel_call(): pl.pallas_call(body, name=name, out_shape=results, in_specs=[spec[n in hb...]
    all_to_all x3, blocking collectives: 35.8 us -> 34.7 us  [exchange(): moved = lax.all_to_all(slots, AXES, split_axis=0, concat_axis=0, tiled=True)]
    all_to_all x1, waiting for transfers between devices: 3.85 us -> 4.72 us  [exchange(): moved = lax.all_to_all(slots, AXES, split_axis=0, concat_axis=0, tiled=True)]
  transfers between devices with their start and end apart: 1 -> 1, of which waited for: 1 -> 1; matrix products, arithmetic and copies ran while one was open for 0% -> 0% of each run, Pallas kernels for 8% -> 6%
where the time goes in v4:
time: 51.9 us; the launch traced here: 51.6 us
  blocking collectives  34.7 us (67%)
  Pallas kernels  8.93 us (17%)
  waiting for transfers between devices  4.72 us (9%)
  starting transfers between devices  2.57 us (5%)
  between operations  0.67 us (1%)
    all_to_all x3, blocking collectives, exchange(): moved = lax.all_to_all(slots, AXES, split_axis=0, concat_axis=0, tiled=True)  34.7 us
    pallas_call x6, Pallas kernels, kernel_call(): pl.pallas_call(body, name=name, out_shape=results, in_specs=[spec[n in hb...  8.93 us
    all_to_all x1, waiting for transfers between devices, exchange(): moved = lax.all_to_all(slots, AXES, split_axis=0, concat_axis=0, tiled=True)  4.72 us
    all_to_all x1, starting transfers between devices, exchange(): moved = lax.all_to_all(slots, AXES, split_axis=0, concat_axis=0, tiled=True)  2.57 us
  transfers between devices with their start and end apart: 1, of which 1 were waited for; matrix products, arithmetic and copies ran while one was open for 0% of the time, Pallas kernels for 6%

profile of v4, /device:TPU:0, one launch (start us, length us, event | category | flops | bytes accessed | tf_op | source)
XLA Modules:
  0.0 51.6 jit_solution(14154210911168330865)
XLA Ops:
  0.6 1.1 %pack_state.1 = (f32[256,128]{1,0:T(8,128)S(1)}, bf16[2,128,256]{2,1,0:T(8,128)(2,1)S(1)}) custom-call(s32[4,4]{1,0:T(4,128)} %nbr_hbm.1, s32[4,4]{1,0:T(4,128)} %face_hbm.1, s32[1,256]{1,0:T(1,128)} %order_hbm.1, f32[4,4,16,72]{3,2,1,0:T(8,128)} %state_hbm.1, bf16[2,128,256]{2,1,0:T(8,128)(2,1)} %constant.2.clone.weight_hbm), custom_call_target="tpu_custom_call" | custom-call | tf_op jit(solution)/shard_map/pack_state/pallas_call | solution.py:624
  1.8 15.5 %all_to_all.20 = f32[32,8,1,128]{3,1,2,0:T(8,128)S(1)} all-to-all(f32[32,8,1,128]{3,1,2,0:T(8,128)S(1)} %bitcast.22), channel_id=1, replica_groups=mesh['cols'=8,'vars'=4] {'cols','vars'}, dimensions={0} | all-to-all | bytes 262144 | tf_op jit(solution)/shard_map/all_to_all | solution.py:638
  17.3 1.4 %tendency.1 = (f32[192,128]{1,0:T(8,128)}, f32[16,2,8,128]{3,2,1,0:T(8,128)S(1)}) custom-call(f32[256,128]{1,0:T(8,128)S(1)} %bitcast.17, bf16[2,128,256]{2,1,0:T(8,128)(2,1)S(1)} %get-tuple-element.15.weight_ref), custom_call_target="tpu_custom_call" | custom-call | tf_op jit(solution)/shard_map/tendency/pallas_call | solution.py:624
  18.7 2.6 %all-to-all-start.1 = ((f32[32,6,1,128]{3,2,1,0:T(1,128)}), f32[32,6,1,128]{3,2,1,0:T(1,128)S(1)}, u32[]{:S(2)}, u32[]{:S(2)}) async-start(f32[32,6,1,128]{3,2,1,0:T(1,128)} %bitcast.3), calls=%async_computation.1 | async-start | bytes 196608 | tf_op jit(solution)/shard_map/all_to_all | solution.py:638
  21.3 3.2 %settle.1 = (f32[16,4,56,128]{3,2,1,0:T(8,128)S(1)}, f32[2,56,128]{2,1,0:T(8,128)S(1)}, bf16[2,1024,128]{2,1,0:T(8,128)(2,1)S(1)}, bf16[256,256]{1,0:T(8,128)(2,...) custom-call(f32[50,16,4,128]{3,2,1,0:T(4,128)} %bitcast.24, f32[50,72]{1,0:T(8,128)} %down_hbm.1, f32[50,72]{1,0:T(8,128)} %bitcast.25), custom_call_target="tpu_custom_call" | custom-call | flops 100000000 | bytes 4000000 | tf_op jit(solution)/shard_map/settle/pallas_call | solution.py:624
  24.5 4.7 %all-to-all-done.1 = f32[32,6,1,128]{3,2,1,0:T(1,128)S(1)} async-done(((f32[32,6,1,128]{3,2,1,0:T(1,128)}), f32[32,6,1,128]{3,2,1,0:T(1,128)S(1)}, u32[]{:S(2)}, u32[]{:S(2)}) %all-to-all-start.1) | async-done | bytes 98336 | tf_op jit(solution)/shard_map/all_to_all | solution.py:638
  29.2 2.0 %cloud.1 = (f32[50,16,4,128]{3,2,1,0:T(4,128)}, f32[192,128]{1,0:T(8,128)S(1)}) custom-call(f32[192,128]{1,0:T(8,128)S(1)} %bitcast.21, f32[16,4,56,128]{3,2,1,0:T(8,128)S(1)} %get-tuple-element.17.base_ref, f32[2,56,128]{2,1,0:T(8,128)S(1)} %get-tuple-element.18.mean_ref, bf16[2,1024,128]{2,1,0:T(8,128)(2,1)S(1)} %get-tuple-element.19.pool_ref, ...), custom_call_target="tpu_custom_call" | custom-call | tf_op jit(solution)/shard_map/cloud/pallas_call | solution.py:624
  31.2 9.6 %all_to_all.21 = f32[32,6,1,128]{3,2,1,0:T(1,128)S(1)} all-to-all(f32[32,6,1,128]{3,2,1,0:T(1,128)S(1)} %bitcast.23), channel_id=1, replica_groups=mesh['cols'=8,'vars'=4] {'cols','vars'}, dimensions={0} | all-to-all | bytes 196608 | tf_op jit(solution)/shard_map/all_to_all | solution.py:638
  40.8 0.5 update.1
  41.3 9.6 %all_to_all.22 = f32[32,6,1,128]{3,2,1,0:T(1,128)S(1)} all-to-all(f32[32,6,1,128]{3,2,1,0:T(1,128)S(1)} %bitcast.20), channel_id=1, replica_groups=mesh['cols'=8,'vars'=4] {'cols','vars'}, dimensions={0} | all-to-all | bytes 196608 | tf_op jit(solution)/shard_map/all_to_all | solution.py:638
  50.9 0.8 %unpack_state.1 = f32[4,4,16,72]{3,2,1,0:T(8,128)} custom-call(f32[192,128]{1,0:T(8,128)S(1)} %bitcast.18), custom_call_target="tpu_custom_call" | custom-call | tf_op jit(solution)/shard_map/unpack_state/pallas_call | solution.py:624
Async XLA Ops:
  18.7 10.5 %all-to-all-start.1 = ((f32[32,6,1,128]{3,2,1,0:T(1,128)}), f32[32,6,1,128]{3,2,1,0:T(1,128)S(1)}, u32[]{:S(2)}, u32[]{:S(2)}) async-start(f32[32,6,1,128]{3,2,1,0:T(1,128)} %bitcast.3), calls=%async_computation.1 | async-start | bytes 196608 | tf_op jit(solution)/shard_map/all_to_all | solution.py:638

commit v5 on v4

--- a/solution.py
+++ b/solution.py
@@ -30,8 +30,6 @@
 PIECE = 2
 GROUP = 16
 SWAPS = 4
-FAR_ROW = 6
-ORDER_ROW = 7
 
 
 def lobatto_derivative():
@@ -122,6 +120,63 @@
     return jnp.broadcast_to(values[row : row + 1], (ROWS, LANES))
 
 
+def far_row(whole):
+    return 2 * whole + 1
+
+
+def order_row(whole):
+    return 2 * whole + 2
+
+
+def scatter_levels(out_ref, pitch, whole, parts, with_wind=False):
+    devices = out_ref.shape[0] // pitch
+    levels = parts[0].shape[0]
+    for pair in range(2):
+        for turn in range(whole):
+            for first in range(0, devices, ROWS):
+                begin = turn * devices + first
+                out_ref[pl.ds(pitch * first + 2 * turn + pair, ROWS, stride=pitch), :] = parts[
+                    pair
+                ][begin : begin + ROWS]
+    for first in range(whole * devices, levels, ROWS):
+        wind = parts[1][first : first + ROWS]
+        for variable in range(4):
+            values = parts[variable % 2][first : first + ROWS]
+            if variable >= 2:
+                values = half_turn(values)
+            if with_wind:
+                values = jnp.where(lane_ids() < LANES // 2, values, wind)
+            begin = pitch * (4 * (first - whole * devices) + variable) + 2 * whole
+            out_ref[pl.ds(begin, ROWS, stride=4 * pitch), :] = values
+
+
+def gather_levels(got_ref, whole, levels):
+    pitch = 2 * whole + 1
+    devices = got_ref.shape[0] // pitch
+    parts = []
+    for pair in range(2):
+        pieces = [
+            got_ref[pl.ds(pitch * first + 2 * turn + pair, ROWS, stride=pitch), :]
+            for turn in range(whole)
+            for first in range(0, devices, ROWS)
+        ]
+        for first in range(whole * devices, levels, ROWS):
+            lower, upper = (
+                got_ref[
+                    pl.ds(
+                        pitch * (4 * (first - whole * devices) + variable) + 2 * whole,
+                        ROWS,
+                        stride=4 * pitch,
+                    ),
+                    :,
+                ]
+                for variable in (pair, 2 + pair)
+            )
+            pieces.append(jnp.where(lane_ids() < LANES // 2, lower, half_turn(upper)))
+        parts.append(jnp.concatenate(pieces, axis=0))
+    return parts
+
+
 def unpack_pairs(got_ref, field):
     rows = got_ref.shape[0] // (2 * field.shape[0])
 
@@ -191,7 +246,7 @@
     state_ref,
     scratch,
     sems,
-    depth,
+    whole,
     block,
 ):
     copies = [
@@ -209,7 +264,6 @@
     for copy in copies:
         copy.start()
     elements, variables, nodes, levels = state_ref.shape
-    used = levels // depth
     half = LANES // 2
     lane = lane_ids()
     own = lax.axis_index("vars")
@@ -262,11 +316,13 @@
     place_part = jnp.where(odd, place_part, half_turn(place_part))
     indices = jnp.where(upper, place_part, order_part)
 
-    slots = out_ref.shape[0] // ROWS
+    pitch = order_row(whole) + 1
+    slots = out_ref.shape[0] // pitch
     for first in range(0, slots, ROWS):
-        out_ref[pl.ds(ROWS * first + FAR_ROW, ROWS, stride=ROWS), :] = far_col
-        out_ref[pl.ds(ROWS * first + ORDER_ROW, ROWS, stride=ROWS), :] = indices
+        out_ref[pl.ds(pitch * first + far_row(whole), ROWS, stride=pitch), :] = far_col
+        out_ref[pl.ds(pitch * first + order_row(whole), ROWS, stride=pitch), :] = indices
     copies[3].wait()
+    parts = []
     for pair in range(variables // 2):
         fields = jnp.concatenate(
             [
@@ -275,22 +331,18 @@
             ],
             axis=0,
         )
-        by_level = fields.T
-        for part in range(depth):
-            for first in range(0, used, ROWS):
-                begin = used * part + first
-                out_ref[pl.ds(ROWS * first + depth * pair + part, ROWS, stride=ROWS), :] = (
-                    by_level[begin : begin + ROWS]
-                )
+        parts.append(fields.T)
+    scatter_levels(out_ref, pitch, whole, parts, with_wind=True)
     copies[4].wait()
 
 
 def tendency_kernel(
-    got_ref, weight_ref, out_ref, partial_ref, field, linear, tend, moved, depth, share
+    got_ref, weight_ref, out_ref, partial_ref, field, linear, tend, moved, whole, share
 ):
     tiles = field.shape[0]
     row = row_ids()
     lower = lane_ids() < LANES // 2
+    wind_row = jnp.where(row < 2 * whole, row | 1, 2 * whole)
     unpack_pairs(got_ref, field)
     step = min(tiles, 16)
 
@@ -311,10 +363,10 @@
         before = jnp.where(q == 0, tiles - 1, q - 1)
         after = jnp.where(q == tiles - 1, 0, q + 1)
         high = field[q, 1]
-        wind = jnp.where(row < depth, pltpu.roll(high, ROWS - depth, 0), high)
+        wind = jnp.take_along_axis(high, wind_row, axis=0, mode="promise_in_bounds")
         sums = [0.0, 0.0]
         for side in range(2):
-            far = row_of(field[q, side], FAR_ROW).astype(jnp.int32)
+            far = row_of(field[q, side], far_row(whole)).astype(jnp.int32)
             spot = far & (LANES - 1)
             inside = lax.shift_right_arithmetic(far, 7) == q
             for part in range(2):
@@ -329,14 +381,16 @@
                 + PENALTY * sums[part]
             )
             tend[q, part] = result
-            partial_ref[q, part] = jnp.where(row < FAR_ROW, own + TIME_STEP * result, own)
+            partial_ref[q, part] = jnp.where(
+                row < far_row(whole), own + TIME_STEP * result, own
+            )
 
     each(tiles, advance)
     swap_groups(tend, moved, share)
 
     def arrange(p):
-        order = row_of(field[p, 0], ORDER_ROW).astype(jnp.int32)
-        pack_pair(out_ref, p, 2 * depth, *reorder(moved, p // 2 * 2, order))
+        order = row_of(field[p, 0], order_row(whole)).astype(jnp.int32)
+        pack_pair(out_ref, p, far_row(whole), *reorder(moved, p // 2 * 2, order))
 
     each(tiles, arrange)
 
@@ -472,30 +526,15 @@
     sums,
     next_ref,
     sem,
-    depth,
+    whole,
 ):
     columns, variables, deep = base_ref.shape[:3]
     clev, levels = down_ref.shape
     plane = (columns + 1) * variables
     flat_ref = next_ref.reshape(clev * plane, LANES)
     steps = columns // WIDE
-    used = levels // depth
-    rows = 2 * depth
     half = LANES // 2
-    fields = jnp.concatenate(
-        [
-            jnp.concatenate(
-                [
-                    got_ref[pl.ds(rows * first + depth * pair + part, ROWS, stride=rows), :]
-                    for part in range(depth)
-                    for first in range(0, used, ROWS)
-                ],
-                axis=0,
-            )
-            for pair in range(2)
-        ],
-        axis=1,
-    )
+    fields = jnp.concatenate(gather_levels(got_ref, whole, levels), axis=1)
     forcing = jnp.dot(TIME_STEP * down_ref[...], fields, precision=EXACT)
     for pair in range(2):
         forced[pair, 0:clev] = forcing[:, LANES * pair : LANES * pair + LANES]
@@ -563,23 +602,22 @@
         (((0,), (0,)), ((), ())),
         precision=EXACT,
     )
-    for pair in range(2):
-        for part in range(depth):
-            for first in range(0, used, ROWS):
-                begin = used * part + first
-                out_ref[pl.ds(rows * first + depth * pair + part, ROWS, stride=rows), :] = (
-                    feedback[begin : begin + ROWS, LANES * pair : LANES * pair + LANES]
-                )
+    scatter_levels(
+        out_ref,
+        far_row(whole),
+        whole,
+        [feedback[:, LANES * pair : LANES * pair + LANES] for pair in range(2)],
+    )
     store(0, columns).wait()
 
 
-def update_kernel(got_ref, partial_ref, out_ref, field, sorted_ref, share):
+def update_kernel(got_ref, partial_ref, out_ref, field, sorted_ref, whole, share):
     tiles = field.shape[0]
     rows = got_ref.shape[0] // (2 * tiles)
     unpack_pairs(got_ref, field)
 
     def collect(p):
-        place = row_of(partial_ref[p, 1], ORDER_ROW).astype(jnp.int32)
+        place = row_of(partial_ref[p, 1], order_row(whole)).astype(jnp.int32)
         for part, values in enumerate(reorder(field, p // 2 * 2, place)):
             sorted_ref[p, part] = values
 
@@ -598,18 +636,9 @@
     each(tiles, finish)
 
 
-def unpack_kernel(got_ref, state_ref, depth):
+def unpack_kernel(got_ref, state_ref, whole):
     elements, variables, nodes, levels = state_ref.shape
-    used = levels // depth
-    for pair in range(variables // 2):
-        by_level = jnp.concatenate(
-            [
-                got_ref[pl.ds(2 * depth * first + depth * pair + part, ROWS, stride=2 * depth), :]
-                for part in range(depth)
-                for first in range(0, used, ROWS)
-            ],
-            axis=0,
-        )
+    for pair, by_level in enumerate(gather_levels(got_ref, whole, levels)):
         fields = by_level.T.reshape(2, elements, nodes, levels)
         state_ref[:, pair] = fields[0]
         state_ref[:, variables // 2 + pair] = fields[1]
@@ -653,14 +682,16 @@
     devices = lax.axis_size(AXES)
     block = column_order.shape[1]
     share = block // lax.axis_size("cols")
-    depth = -(-levels // devices)
+    whole = levels // devices
+    left = levels - whole * devices
     assert variables == 4 and nodes == NODES and 2 * elements * nodes == LANES
-    assert 2 * depth <= FAR_ROW and levels % (ROWS * depth) == 0 and block == 2 * LANES
+    assert variables * left <= devices and left % ROWS == 0 and devices % ROWS == 0
+    assert order_row(whole) < ROWS and block == 2 * LANES
     tiles = devices // 2
     f32 = jnp.float32
     shape = jax.ShapeDtypeStruct
-    flat = shape((devices * ROWS, LANES), f32)
-    rows = shape((devices * 2 * depth, LANES), f32)
+    flat = shape((devices * (order_row(whole) + 1), LANES), f32)
+    rows = shape((devices * far_row(whole), LANES), f32)
     pairs = shape((tiles, 2, ROWS, LANES), f32)
     columns = width // LANES
     assert columns % WIDE == 0 and WIDE % PIECE == 0
@@ -668,7 +699,7 @@
     dma = pltpu.SemaphoreType.DMA
 
     packed, weights = kernel_call(
-        functools.partial(pack_kernel, depth=depth, block=block),
+        functools.partial(pack_kernel, whole=whole, block=block),
         "pack_state",
         (flat, shape((2, LANES, 2 * LANES), jnp.bfloat16)),
         [
@@ -688,7 +719,7 @@
     )
     by_level = exchange(packed, devices)
     arranged, partial = kernel_call(
-        functools.partial(tendency_kernel, depth=depth, share=share),
+        functools.partial(tendency_kernel, whole=whole, share=share),
         "tendency",
         (rows, pairs),
         [
@@ -725,7 +756,7 @@
     )
     by_column = exchange(arranged, devices)
     cloud_next, fed = kernel_call(
-        functools.partial(cloud_kernel, depth=depth),
+        functools.partial(cloud_kernel, whole=whole),
         "cloud",
         (shape(by_tile.shape, f32), rows),
         [
@@ -745,7 +776,7 @@
     )
     fed_level = exchange(fed, devices)
     (advanced,) = kernel_call(
-        functools.partial(update_kernel, share=share),
+        functools.partial(update_kernel, whole=whole, share=share),
         "update",
         (rows,),
         [pltpu.VMEM(pairs.shape, f32), pltpu.VMEM(pairs.shape, f32)],
@@ -754,7 +785,7 @@
     )
     home = exchange(advanced, devices)
     (model_next,) = kernel_call(
-        functools.partial(unpack_kernel, depth=depth),
+        functools.partial(unpack_kernel, whole=whole),
         "unpack_state",
         (shape(model_state.shape, f32),),
         [],

time: 51.9 us -> 51.1 us (0.985)
  blocking collectives: 34.7 us -> 34 us
    all_to_all x3, blocking collectives: 34.7 us -> 34 us  [exchange(): moved = lax.all_to_all(slots, AXES, split_axis=0, concat_axis=0, tiled=True)]
where the time goes in v5:
time: 51.1 us; the launch traced here: 50.9 us
  blocking collectives  34 us (67%)
  Pallas kernels  9.1 us (18%)
  waiting for transfers between devices  4.49 us (9%)
  starting transfers between devices  2.57 us (5%)
  between operations  0.67 us (1%)
    all_to_all x3, blocking collectives, exchange(): moved = lax.all_to_all(slots, AXES, split_axis=0, concat_axis=0, tiled=True)  34 us
    pallas_call x6, Pallas kernels, kernel_call(): pl.pallas_call(body, name=name, out_shape=results, in_specs=[spec[n in hb...  9.1 us
    all_to_all x1, waiting for transfers between devices, exchange(): moved = lax.all_to_all(slots, AXES, split_axis=0, concat_axis=0, tiled=True)  4.49 us
    all_to_all x1, starting transfers between devices, exchange(): moved = lax.all_to_all(slots, AXES, split_axis=0, concat_axis=0, tiled=True)  2.57 us
  transfers between devices with their start and end apart: 1, of which 1 were waited for; matrix products, arithmetic and copies ran while one was open for 0% of the time, Pallas kernels for 6%

profile of v5, /device:TPU:0, one launch (start us, length us, event | category | flops | bytes accessed | tf_op | source)
XLA Modules:
  0.0 50.9 jit_solution(13372212340497920109)
XLA Ops:
  0.6 1.2 %pack_state.1 = (f32[224,128]{1,0:T(8,128)S(1)}, bf16[2,128,256]{2,1,0:T(8,128)(2,1)S(1)}) custom-call(s32[4,4]{1,0:T(4,128)} %nbr_hbm.1, s32[4,4]{1,0:T(4,128)} %face_hbm.1, s32[1,256]{1,0:T(1,128)} %order_hbm.1, f32[4,4,16,72]{3,2,1,0:T(8,128)} %state_hbm.1, bf16[2,128,256]{2,1,0:T(8,128)(2,1)} %constant.2.clone.weight_hbm), custom_call_target="tpu_custom_call" | custom-call | tf_op jit(solution)/shard_map/pack_state/pallas_call | solution.py:653
  1.8 15.3 %all_to_all.20 = f32[32,7,1,128]{3,2,1,0:T(1,128)S(1)} all-to-all(f32[32,7,1,128]{3,2,1,0:T(1,128)S(1)} %bitcast.20), channel_id=1, replica_groups=mesh['cols'=8,'vars'=4] {'cols','vars'}, dimensions={0} | all-to-all | bytes 229376 | tf_op jit(solution)/shard_map/all_to_all | solution.py:667
  17.1 1.4 %tendency.1 = (f32[160,128]{1,0:T(8,128)}, f32[16,2,8,128]{3,2,1,0:T(8,128)S(1)}) custom-call(f32[224,128]{1,0:T(8,128)S(1)} %bitcast.15, bf16[2,128,256]{2,1,0:T(8,128)(2,1)S(1)} %get-tuple-element.15.weight_ref), custom_call_target="tpu_custom_call" | custom-call | tf_op jit(solution)/shard_map/tendency/pallas_call | solution.py:653
  18.5 2.6 %all-to-all-start.1 = ((f32[32,5,1,128]{3,2,1,0:T(1,128)}), f32[32,5,1,128]{3,2,1,0:T(1,128)S(1)}, u32[]{:S(2)}, u32[]{:S(2)}) async-start(f32[32,5,1,128]{3,2,1,0:T(1,128)} %bitcast.2), calls=%async_computation.1 | async-start | bytes 163840 | tf_op jit(solution)/shard_map/all_to_all | solution.py:667
  21.1 3.2 %settle.1 = (f32[16,4,56,128]{3,2,1,0:T(8,128)S(1)}, f32[2,56,128]{2,1,0:T(8,128)S(1)}, bf16[2,1024,128]{2,1,0:T(8,128)(2,1)S(1)}, bf16[256,256]{1,0:T(8,128)(2,...) custom-call(f32[50,16,4,128]{3,2,1,0:T(4,128)} %bitcast.22, f32[50,72]{1,0:T(8,128)} %down_hbm.1, f32[50,72]{1,0:T(8,128)} %bitcast.23), custom_call_target="tpu_custom_call" | custom-call | flops 100000000 | bytes 4000000 | tf_op jit(solution)/shard_map/settle/pallas_call | solution.py:653
  24.3 4.5 %all-to-all-done.1 = f32[32,5,1,128]{3,2,1,0:T(1,128)S(1)} async-done(((f32[32,5,1,128]{3,2,1,0:T(1,128)}), f32[32,5,1,128]{3,2,1,0:T(1,128)S(1)}, u32[]{:S(2)}, u32[]{:S(2)}) %all-to-all-start.1) | async-done | bytes 81952 | tf_op jit(solution)/shard_map/all_to_all | solution.py:667
  28.8 2.0 %cloud.1 = (f32[50,16,4,128]{3,2,1,0:T(4,128)}, f32[160,128]{1,0:T(8,128)S(1)}) custom-call(f32[160,128]{1,0:T(8,128)S(1)} %bitcast.19, f32[16,4,56,128]{3,2,1,0:T(8,128)S(1)} %get-tuple-element.17.base_ref, f32[2,56,128]{2,1,0:T(8,128)S(1)} %get-tuple-element.18.mean_ref, bf16[2,1024,128]{2,1,0:T(8,128)(2,1)S(1)} %get-tuple-element.19.pool_ref, ...), custom_call_target="tpu_custom_call" | custom-call | tf_op jit(solution)/shard_map/cloud/pallas_call | solution.py:653
  30.9 9.4 %all_to_all.21 = f32[32,5,1,128]{3,2,1,0:T(1,128)S(1)} all-to-all(f32[32,5,1,128]{3,2,1,0:T(1,128)S(1)} %bitcast.21), channel_id=1, replica_groups=mesh['cols'=8,'vars'=4] {'cols','vars'}, dimensions={0} | all-to-all | bytes 163840 | tf_op jit(solution)/shard_map/all_to_all | solution.py:667
  40.2 0.5 update.1
  40.7 9.4 %all_to_all.22 = f32[32,5,1,128]{3,2,1,0:T(1,128)S(1)} all-to-all(f32[32,5,1,128]{3,2,1,0:T(1,128)S(1)} %bitcast.17), channel_id=1, replica_groups=mesh['cols'=8,'vars'=4] {'cols','vars'}, dimensions={0} | all-to-all | bytes 163840 | tf_op jit(solution)/shard_map/all_to_all | solution.py:667
  50.1 0.8 %unpack_state.1 = f32[4,4,16,72]{3,2,1,0:T(8,128)} custom-call(f32[160,128]{1,0:T(8,128)S(1)} %bitcast.18), custom_call_target="tpu_custom_call" | custom-call | tf_op jit(solution)/shard_map/unpack_state/pallas_call | solution.py:653
Async XLA Ops:
  18.5 10.3 %all-to-all-start.1 = ((f32[32,5,1,128]{3,2,1,0:T(1,128)}), f32[32,5,1,128]{3,2,1,0:T(1,128)S(1)}, u32[]{:S(2)}, u32[]{:S(2)}) async-start(f32[32,5,1,128]{3,2,1,0:T(1,128)} %bitcast.2), calls=%async_computation.1 | async-start | bytes 163840 | tf_op jit(solution)/shard_map/all_to_all | solution.py:667

commit v6 on v5

--- a/solution.py
+++ b/solution.py
@@ -337,7 +337,17 @@
 
 
 def tendency_kernel(
-    got_ref, weight_ref, out_ref, partial_ref, field, linear, tend, moved, whole, share
+    got_ref,
+    weight_ref,
+    settled_ref,
+    out_ref,
+    partial_ref,
+    field,
+    linear,
+    tend,
+    moved,
+    whole,
+    share,
 ):
     tiles = field.shape[0]
     row = row_ids()
@@ -718,19 +728,6 @@
         hbm_in=range(5),
     )
     by_level = exchange(packed, devices)
-    arranged, partial = kernel_call(
-        functools.partial(tendency_kernel, whole=whole, share=share),
-        "tendency",
-        (rows, pairs),
-        [
-            pltpu.VMEM(pairs.shape, f32),
-            pltpu.VMEM((tiles, 2, ROWS, 2 * LANES), f32),
-            pltpu.VMEM(pairs.shape, f32),
-            pltpu.VMEM(pairs.shape, f32),
-        ],
-        by_level,
-        weights,
-    )
     by_tile = cloud_state.reshape(variables, clev, columns, LANES).transpose(1, 2, 0, 3)
     base, mean, pool, spread, down, up = kernel_call(
         settle_kernel,
@@ -754,6 +751,20 @@
         hbm_in=range(3),
         cost=pl.CostEstimate(flops=10**8, bytes_accessed=4 * 10**6, transcendentals=0),
     )
+    arranged, partial = kernel_call(
+        functools.partial(tendency_kernel, whole=whole, share=share),
+        "tendency",
+        (rows, pairs),
+        [
+            pltpu.VMEM(pairs.shape, f32),
+            pltpu.VMEM((tiles, 2, ROWS, 2 * LANES), f32),
+            pltpu.VMEM(pairs.shape, f32),
+            pltpu.VMEM(pairs.shape, f32),
+        ],
+        by_level,
+        weights,
+        down,
+    )
     by_column = exchange(arranged, devices)
     cloud_next, fed = kernel_call(
         functools.partial(cloud_kernel, whole=whole),

time: 51.1 us -> 50.5 us (0.988)
  blocking collectives: 34 us -> 28.1 us
  starting transfers between devices: 2.57 us -> 7.33 us
    all_to_all x3, blocking collectives: 34 us -> 28.1 us  [exchange(): moved = lax.all_to_all(slots, AXES, split_axis=0, concat_axis=0, tiled=True)]
    all_to_all x1, starting transfers between devices: 2.57 us -> 7.33 us  [exchange(): moved = lax.all_to_all(slots, AXES, split_axis=0, concat_axis=0, tiled=True)]
where the time goes in v6:
time: 50.5 us; the launch traced here: 50.2 us
  blocking collectives  28.1 us (56%)
  Pallas kernels  9.1 us (18%)
  starting transfers between devices  7.33 us (15%)
  waiting for transfers between devices  4.95 us (10%)
  between operations  0.67 us (1%)
    all_to_all x3, blocking collectives, exchange(): moved = lax.all_to_all(slots, AXES, split_axis=0, concat_axis=0, tiled=True)  28.1 us
    pallas_call x6, Pallas kernels, kernel_call(): pl.pallas_call(body, name=name, out_shape=results, in_specs=[spec[n in hb...  9.1 us
    all_to_all x1, starting transfers between devices, exchange(): moved = lax.all_to_all(slots, AXES, split_axis=0, concat_axis=0, tiled=True)  7.33 us
    all_to_all x1, waiting for transfers between devices, exchange(): moved = lax.all_to_all(slots, AXES, split_axis=0, concat_axis=0, tiled=True)  4.95 us
  transfers between devices with their start and end apart: 1, of which 1 were waited for; matrix products, arithmetic and copies ran while one was open for 0% of the time, Pallas kernels for 6%

profile of v6, /device:TPU:0, one launch (start us, length us, event | category | flops | bytes accessed | tf_op | source)
XLA Modules:
  0.0 50.2 jit_solution(5970750463001258187)
XLA Ops:
  0.6 1.8 %pack_state.1 = (f32[224,128]{1,0:T(8,128)}, bf16[2,128,256]{2,1,0:T(8,128)(2,1)S(1)}) custom-call(s32[4,4]{1,0:T(4,128)} %nbr_hbm.1, s32[4,4]{1,0:T(4,128)} %face_hbm.1, s32[1,256]{1,0:T(1,128)} %order_hbm.1, f32[4,4,16,72]{3,2,1,0:T(8,128)} %state_hbm.1, bf16[2,128,256]{2,1,0:T(8,128)(2,1)} %constant.2.clone.weight_hbm), custom_call_target="tpu_custom_call" | custom-call | tf_op jit(solution)/shard_map/pack_state/pallas_call | solution.py:663
  2.5 7.3 %all-to-all-start = ((f32[32,7,1,128]{3,2,1,0:T(1,128)}), f32[32,7,1,128]{3,2,1,0:T(1,128)S(1)}, u32[]{:S(2)}, u32[]{:S(2)}) async-start(f32[32,7,1,128]{3,2,1,0:T(1,128)} %bitcast), calls=%async_computation | async-start | bytes 229376 | tf_op jit(solution)/shard_map/all_to_all | solution.py:677
  9.8 3.2 %settle.1 = (f32[16,4,56,128]{3,2,1,0:T(8,128)S(1)}, f32[2,56,128]{2,1,0:T(8,128)S(1)}, bf16[2,1024,128]{2,1,0:T(8,128)(2,1)S(1)}, bf16[256,256]{1,0:T(8,128)(2,...) custom-call(f32[50,16,4,128]{3,2,1,0:T(4,128)} %bitcast.22, f32[50,72]{1,0:T(8,128)} %down_hbm.1, f32[50,72]{1,0:T(8,128)} %bitcast.23), custom_call_target="tpu_custom_call" | custom-call | flops 100000000 | bytes 4000000 | tf_op jit(solution)/shard_map/settle/pallas_call | solution.py:663
  13.0 5.0 %all-to-all-done = f32[32,7,1,128]{3,2,1,0:T(1,128)S(1)} async-done(((f32[32,7,1,128]{3,2,1,0:T(1,128)}), f32[32,7,1,128]{3,2,1,0:T(1,128)S(1)}, u32[]{:S(2)}, u32[]{:S(2)}) %all-to-all-start) | async-done | bytes 114720 | tf_op jit(solution)/shard_map/all_to_all | solution.py:677
  18.0 0.8 %tendency.1 = (f32[160,128]{1,0:T(8,128)S(1)}, f32[16,2,8,128]{3,2,1,0:T(8,128)S(1)}) custom-call(f32[224,128]{1,0:T(8,128)S(1)} %bitcast.15, bf16[2,128,256]{2,1,0:T(8,128)(2,1)S(1)} %get-tuple-element.15.weight_ref, f32[50,72]{1,0:T(8,128)S(1)} %get-tuple-element.16.settled_ref.down_ref), custom_call_target="tpu_custom_call" | custom-call | tf_op jit(solution)/shard_map/tendency/pallas_call | solution.py:663
  18.8 9.4 %all_to_all.20 = f32[32,5,1,128]{3,2,1,0:T(1,128)S(1)} all-to-all(f32[32,5,1,128]{3,2,1,0:T(1,128)S(1)} %bitcast.21), channel_id=1, replica_groups=mesh['cols'=8,'vars'=4] {'cols','vars'}, dimensions={0} | all-to-all | bytes 163840 | tf_op jit(solution)/shard_map/all_to_all | solution.py:677
  28.1 2.0 %cloud.1 = (f32[50,16,4,128]{3,2,1,0:T(4,128)}, f32[160,128]{1,0:T(8,128)S(1)}) custom-call(f32[160,128]{1,0:T(8,128)S(1)} %bitcast.19, f32[16,4,56,128]{3,2,1,0:T(8,128)S(1)} %get-tuple-element.18.base_ref, f32[2,56,128]{2,1,0:T(8,128)S(1)} %get-tuple-element.19.mean_ref, bf16[2,1024,128]{2,1,0:T(8,128)(2,1)S(1)} %get-tuple-element.20.pool_ref, ...), custom_call_target="tpu_custom_call" | custom-call | tf_op jit(solution)/shard_map/cloud/pallas_call | solution.py:663
  30.2 9.4 %all_to_all.21 = f32[32,5,1,128]{3,2,1,0:T(1,128)S(1)} all-to-all(f32[32,5,1,128]{3,2,1,0:T(1,128)S(1)} %bitcast.20), channel_id=1, replica_groups=mesh['cols'=8,'vars'=4] {'cols','vars'}, dimensions={0} | all-to-all | bytes 163840 | tf_op jit(solution)/shard_map/all_to_all | solution.py:677
  39.5 0.5 update.1
  40.0 9.4 %all_to_all.22 = f32[32,5,1,128]{3,2,1,0:T(1,128)S(1)} all-to-all(f32[32,5,1,128]{3,2,1,0:T(1,128)S(1)} %bitcast.17), channel_id=1, replica_groups=mesh['cols'=8,'vars'=4] {'cols','vars'}, dimensions={0} | all-to-all | bytes 163840 | tf_op jit(solution)/shard_map/all_to_all | solution.py:677
  49.4 0.8 %unpack_state.1 = f32[4,4,16,72]{3,2,1,0:T(8,128)} custom-call(f32[160,128]{1,0:T(8,128)S(1)} %bitcast.18), custom_call_target="tpu_custom_call" | custom-call | tf_op jit(solution)/shard_map/unpack_state/pallas_call | solution.py:663
Async XLA Ops:
  2.5 15.5 %all-to-all-start = ((f32[32,7,1,128]{3,2,1,0:T(1,128)}), f32[32,7,1,128]{3,2,1,0:T(1,128)S(1)}, u32[]{:S(2)}, u32[]{:S(2)}) async-start(f32[32,7,1,128]{3,2,1,0:T(1,128)} %bitcast), calls=%async_computation | async-start | bytes 229376 | tf_op jit(solution)/shard_map/all_to_all | solution.py:677

commit v7 on v6

--- a/solution.py
+++ b/solution.py
@@ -26,7 +26,7 @@
 LOG2_E = 1.4426950408889634
 EXACT = lax.Precision.HIGHEST
 KERNEL_VMEM = 16 * 2**20
-WIDE = 8
+WIDE = 16
 PIECE = 2
 GROUP = 16
 SWAPS = 4
@@ -411,6 +411,15 @@
     return high, low
 
 
+def three_products(left, right, dims):
+    left_high, left_low = in_two(left)
+    right_high, right_low = in_two(right)
+    return sum(
+        lax.dot_general(a, b, (dims, ((), ())), preferred_element_type=jnp.float32)
+        for a, b in ((left_high, right_high), (left_high, right_low), (left_low, right_high))
+    )
+
+
 def pool_weights(step):
     wide = WIDE * LANES
     lane = lax.broadcasted_iota(jnp.int32, (wide, LANES), 1) % (LANES // 2)
@@ -545,7 +554,7 @@
     steps = columns // WIDE
     half = LANES // 2
     fields = jnp.concatenate(gather_levels(got_ref, whole, levels), axis=1)
-    forcing = jnp.dot(TIME_STEP * down_ref[...], fields, precision=EXACT)
+    forcing = three_products(TIME_STEP * down_ref[...], fields, ((1,), (0,)))
     for pair in range(2):
         forced[pair, 0:clev] = forcing[:, LANES * pair : LANES * pair + LANES]
         forced[pair, clev:deep] = jnp.zeros((deep - clev, LANES), jnp.float32)
@@ -606,11 +615,8 @@
     first = mean_ref[0, 0:clev] + jnp.where(lower, share, share * RETAIN) * forced[0, 0:clev]
     first = first + extra
     second = mean_ref[1, 0:clev] + share * forced[1, 0:clev] - jnp.where(lower, extra, 0.0)
-    feedback = lax.dot_general(
-        up_ref[...],
-        jnp.concatenate([first, second], axis=1),
-        (((0,), (0,)), ((), ())),
-        precision=EXACT,
+    feedback = three_products(
+        up_ref[...], jnp.concatenate([first, second], axis=1), ((0,), (0,))
     )
     scatter_levels(
         out_ref,

time: 50.5 us -> 50.1 us (level)
  no operation moved by 1% of the time
where the time goes in v7:
time: 50.1 us; the launch traced here: 49.8 us
  blocking collectives  28.1 us (56%)
  Pallas kernels  8.62 us (17%)
  starting transfers between devices  7.33 us (15%)
  waiting for transfers between devices  5.06 us (10%)
  between operations  0.67 us (1%)
    all_to_all x3, blocking collectives, exchange(): moved = lax.all_to_all(slots, AXES, split_axis=0, concat_axis=0, tiled=True)  28.1 us
    pallas_call x6, Pallas kernels, kernel_call(): pl.pallas_call(body, name=name, out_shape=results, in_specs=[spec[n in hb...  8.62 us
    all_to_all x1, starting transfers between devices, exchange(): moved = lax.all_to_all(slots, AXES, split_axis=0, concat_axis=0, tiled=True)  7.33 us
    all_to_all x1, waiting for transfers between devices, exchange(): moved = lax.all_to_all(slots, AXES, split_axis=0, concat_axis=0, tiled=True)  5.06 us
  transfers between devices with their start and end apart: 1, of which 1 were waited for; matrix products, arithmetic and copies ran while one was open for 0% of the time, Pallas kernels for 6%

profile of v7, /device:TPU:0, one launch (start us, length us, event | category | flops | bytes accessed | tf_op | source)
XLA Modules:
  0.0 49.8 jit_solution(9245291582052288917)
XLA Ops:
  0.6 1.8 %pack_state.1 = (f32[224,128]{1,0:T(8,128)}, bf16[2,128,256]{2,1,0:T(8,128)(2,1)S(1)}) custom-call(s32[4,4]{1,0:T(4,128)} %nbr_hbm.1, s32[4,4]{1,0:T(4,128)} %face_hbm.1, s32[1,256]{1,0:T(1,128)} %order_hbm.1, f32[4,4,16,72]{3,2,1,0:T(8,128)} %state_hbm.1, bf16[2,128,256]{2,1,0:T(8,128)(2,1)} %constant.2.clone.weight_hbm), custom_call_target="tpu_custom_call" | custom-call | tf_op jit(solution)/shard_map/pack_state/pallas_call | solution.py:669
  2.5 7.3 %all-to-all-start = ((f32[32,7,1,128]{3,2,1,0:T(1,128)}), f32[32,7,1,128]{3,2,1,0:T(1,128)S(1)}, u32[]{:S(2)}, u32[]{:S(2)}) async-start(f32[32,7,1,128]{3,2,1,0:T(1,128)} %bitcast), calls=%async_computation | async-start | bytes 229376 | tf_op jit(solution)/shard_map/all_to_all | solution.py:683
  9.8 3.1 %settle.1 = (f32[16,4,56,128]{3,2,1,0:T(8,128)S(1)}, f32[2,56,128]{2,1,0:T(8,128)S(1)}, bf16[1,2048,128]{2,1,0:T(8,128)(2,1)S(1)}, bf16[256,256]{1,0:T(8,128)(2,...) custom-call(f32[50,16,4,128]{3,2,1,0:T(4,128)} %bitcast.22, f32[50,72]{1,0:T(8,128)} %down_hbm.1, f32[50,72]{1,0:T(8,128)} %bitcast.23), custom_call_target="tpu_custom_call" | custom-call | flops 100000000 | bytes 4000000 | tf_op jit(solution)/shard_map/settle/pallas_call | solution.py:669
  12.9 5.1 %all-to-all-done = f32[32,7,1,128]{3,2,1,0:T(1,128)S(1)} async-done(((f32[32,7,1,128]{3,2,1,0:T(1,128)}), f32[32,7,1,128]{3,2,1,0:T(1,128)S(1)}, u32[]{:S(2)}, u32[]{:S(2)}) %all-to-all-start) | async-done | bytes 114720 | tf_op jit(solution)/shard_map/all_to_all | solution.py:683
  18.0 0.8 %tendency.1 = (f32[160,128]{1,0:T(8,128)S(1)}, f32[16,2,8,128]{3,2,1,0:T(8,128)S(1)}) custom-call(f32[224,128]{1,0:T(8,128)S(1)} %bitcast.15, bf16[2,128,256]{2,1,0:T(8,128)(2,1)S(1)} %get-tuple-element.15.weight_ref, f32[50,72]{1,0:T(8,128)S(1)} %get-tuple-element.16.settled_ref.down_ref), custom_call_target="tpu_custom_call" | custom-call | tf_op jit(solution)/shard_map/tendency/pallas_call | solution.py:669
  18.8 9.4 %all_to_all.20 = f32[32,5,1,128]{3,2,1,0:T(1,128)S(1)} all-to-all(f32[32,5,1,128]{3,2,1,0:T(1,128)S(1)} %bitcast.21), channel_id=1, replica_groups=mesh['cols'=8,'vars'=4] {'cols','vars'}, dimensions={0} | all-to-all | bytes 163840 | tf_op jit(solution)/shard_map/all_to_all | solution.py:683
  28.1 1.7 %cloud.1 = (f32[50,16,4,128]{3,2,1,0:T(4,128)}, f32[160,128]{1,0:T(8,128)S(1)}) custom-call(f32[160,128]{1,0:T(8,128)S(1)} %bitcast.19, f32[16,4,56,128]{3,2,1,0:T(8,128)S(1)} %get-tuple-element.18.base_ref, f32[2,56,128]{2,1,0:T(8,128)S(1)} %get-tuple-element.19.mean_ref, bf16[1,2048,128]{2,1,0:T(8,128)(2,1)S(1)} %get-tuple-element.20.pool_ref, ...), custom_call_target="tpu_custom_call" | custom-call | tf_op jit(solution)/shard_map/cloud/pallas_call | solution.py:669
  29.8 9.4 %all_to_all.21 = f32[32,5,1,128]{3,2,1,0:T(1,128)S(1)} all-to-all(f32[32,5,1,128]{3,2,1,0:T(1,128)S(1)} %bitcast.20), channel_id=1, replica_groups=mesh['cols'=8,'vars'=4] {'cols','vars'}, dimensions={0} | all-to-all | bytes 163840 | tf_op jit(solution)/shard_map/all_to_all | solution.py:683
  39.2 0.5 update.1
  39.6 9.4 %all_to_all.22 = f32[32,5,1,128]{3,2,1,0:T(1,128)S(1)} all-to-all(f32[32,5,1,128]{3,2,1,0:T(1,128)S(1)} %bitcast.17), channel_id=1, replica_groups=mesh['cols'=8,'vars'=4] {'cols','vars'}, dimensions={0} | all-to-all | bytes 163840 | tf_op jit(solution)/shard_map/all_to_all | solution.py:683
  49.0 0.8 %unpack_state.1 = f32[4,4,16,72]{3,2,1,0:T(8,128)} custom-call(f32[160,128]{1,0:T(8,128)S(1)} %bitcast.18), custom_call_target="tpu_custom_call" | custom-call | tf_op jit(solution)/shard_map/unpack_state/pallas_call | solution.py:669
Async XLA Ops:
  2.5 15.5 %all-to-all-start = ((f32[32,7,1,128]{3,2,1,0:T(1,128)}), f32[32,7,1,128]{3,2,1,0:T(1,128)S(1)}, u32[]{:S(2)}, u32[]{:S(2)}) async-start(f32[32,7,1,128]{3,2,1,0:T(1,128)} %bitcast), calls=%async_computation | async-start | bytes 229376 | tf_op jit(solution)/shard_map/all_to_all | solution.py:683
